TPU v7x, 32 devices: a whole 2x2x4 slice. The times are simulated.
32 devices in a mesh: parts: 2 (over y), dp: 4 (over x, core), tp: 4 (over z).
Axes of the slice: x: 2, y: 2, z: 4, core: 2. Of those that a mesh axis runs over, the one named last changes fastest.
Arguments:
- hidden: bfloat16 [32, 128, 8192], P(('parts', 'dp'), 'tp'), parts along dimension 0, may hold values from -6 to 6
- norm_gain: bfloat16 [8192], replicated, may hold values from 0.099609375 to 1.8984375
- w_query: bfloat16 [8192, 4096], P(None, 'tp'), may hold values from -0.0625 to 0.0625
- w_keyval: bfloat16 [8192, 1024], P(None, 'tp'), may hold values from -0.0625 to 0.0625
- w_out: bfloat16 [4096, 8192], P('tp'), may hold values from -0.5 to 0.5
- kv_cache: bfloat16 [1024, 16, 32, 256], P(('parts', 'dp'), 'tp'), parts along dimension 0, may hold values from -600 to 600
- page_table: int32 [32, 32], P(('parts', 'dp')), parts along dimension 0, may hold values from 0 to 127, as said below
- prefix_len: int32 [32], P(('parts', 'dp')), parts along dimension 0, may hold values from 0 to 4096, as said below
- live_rows: int32 [32], P(('parts', 'dp')), parts along dimension 0, may hold values from 1 to 128
- plan: int32 [32], P(('parts', 'dp')), parts along dimension 0, may hold values from 0 to 3, as said below
Outputs:
- result: bfloat16 [32, 128, 8192], P(('parts', 'dp'), 'tp'), parts along dimension 0
- new_kv: bfloat16 [32, 128, 1024], P(('parts', 'dp'), None, 'tp'), parts along dimension 0
There are 2 independent parts, one for each index of `parts`. A program takes and returns all parts, laid end to end along the dimension named above; an argument that names none is the same for every part. Nothing has to cross between parts.
Inputs may be any that keep to these rules, and one draw needn't show every extreme that they name: `page_table`: the 32 pages listed for a stretch belong to its own group, and no page is listed twice within a group. `prefix_len`: a multiple of 128; within a group it never grows with the slot number. `plan`: the 4 stretches of one group go to different groups, and every group receives exactly one stretch of each slot number.
All inputs are finite; a program needn't handle non-finite values.
Results may differ from a plain program's by a relative error of at most 0.02.
The roundings to bfloat16 on the way count: a program that leaves them out, or rounds other values in their place, can miss the bound.
Values may be sent and summed in bfloat16 or wider, within the bound.
No kernel may reach another device: no remote copies, remote signals or barrier semaphores. Data moves between devices by JAX's collectives and lax.ppermute only.
A program may use at most 128 MiB of HBM per device.

v0:
```python
import math

import jax
import jax.numpy as jnp
from jax import lax
from jax.sharding import PartitionSpec as P

KV_HEADS = 4
HEAD_DIM = 128
BLOCK = 128
MAX_PAGES = 32


EPSILON = 1e-05
ROPE_BASE = 500000.0
MASKED = -1e30


def from_partner(value, axis, distance):
    mask = 2**distance
    pairs = [(source, source ^ mask) for source in range(lax.axis_size(axis))]
    return lax.ppermute(value, axis, pairs)


def rotate(values, positions):
    half_width = values.shape[-1] // 2
    frequency = ROPE_BASE ** (-jnp.arange(half_width, dtype=jnp.float32) / half_width)
    angles = positions.astype(jnp.float32)[..., None] * frequency
    cosine = jnp.cos(angles)[..., None, :]
    sine_values = jnp.sin(angles)[..., None, :]
    front_half = values[..., :half_width]
    back_half = values[..., half_width:]
    return jnp.concatenate(
        [
            front_half * cosine - back_half * sine_values,
            back_half * cosine + front_half * sine_values,
        ],
        axis=-1,
    )


def attend_one(inputs):
    queries, head_pairs, prefix, start, count = inputs
    head_width = queries.shape[-1]
    scaling = 1.0 / math.sqrt(head_width)
    row_count = queries.shape[0]
    row_index = jnp.arange(row_count, dtype=jnp.int32)
    own_mask = (row_index[None, :] <= row_index[:, None]) & (row_index[None, :] < count)
    own_scores = (
        jnp.einsum(
            "chd,jd->hcj", queries, head_pairs[:, :head_width], preferred_element_type=jnp.float32
        )
        * scaling
    )
    own_scores = jnp.where(own_mask[None], own_scores, MASKED)
    span_pages = max(1, min(MAX_PAGES, 512 // BLOCK))
    key_span = span_pages * BLOCK
    block_count = (start + key_span - 1) // key_span

    def block_scores(block_id):
        key_block = lax.dynamic_slice_in_dim(prefix, block_id * key_span, key_span, 0)
        scores = (
            jnp.einsum(
                "chd,td->hct",
                queries,
                key_block[:, :head_width],
                preferred_element_type=jnp.float32,
            )
            * scaling
        )
        key_place = block_id * key_span + jnp.arange(key_span, dtype=jnp.int32)
        key_mask = key_place < start
        return (jnp.where(key_mask[None, None, :], scores, MASKED), key_block)

    running_max = jnp.max(own_scores, axis=-1)
    running_sum = jnp.sum(jnp.exp(own_scores - running_max[..., None]), axis=-1)

    def first_pass(block_id, state_pair):
        old_max, old_sum = state_pair
        scores, key_block = block_scores(block_id)
        raised_max = jnp.maximum(old_max, jnp.max(scores, axis=-1))
        new_sum = old_sum * jnp.exp(old_max - raised_max) + jnp.sum(
            jnp.exp(scores - raised_max[..., None]), axis=-1
        )
        return (raised_max, new_sum)

    running_max, running_sum = lax.fori_loop(0, block_count, first_pass, (running_max, running_sum))

    def normalize(scores):
        return (jnp.exp(scores - running_max[..., None]) / running_sum[..., None]).astype(
            jnp.bfloat16
        )

    attended = jnp.einsum(
        "hcj,jd->chd",
        normalize(own_scores),
        head_pairs[:, head_width:],
        preferred_element_type=jnp.float32,
    )

    def second_pass(block_id, gathered_sum):
        scores, key_block = block_scores(block_id)
        return gathered_sum + jnp.einsum(
            "hct,td->chd",
            normalize(scores),
            key_block[:, head_width:],
            preferred_element_type=jnp.float32,
        )

    attended = lax.fori_loop(0, block_count, second_pass, attended)
    return attended.astype(jnp.bfloat16)


def attend(queries, head_pairs, prefix, starts, counts):
    return lax.map(attend_one, (queries, head_pairs, prefix, starts, counts))


def layer(stretch_rows, stretch_pages, starts, counts, norm_gain, w_query, w_keyval, w_out):
    tensor_size = lax.axis_size("tp")
    tensor_rank = lax.axis_index("tp")
    widened = stretch_rows.astype(jnp.float32)
    normed = (
        widened
        * lax.rsqrt(jnp.mean(widened * widened, axis=-1, keepdims=True) + EPSILON)
        * norm_gain.astype(jnp.float32)
    ).astype(jnp.bfloat16)
    query_width = w_query.shape[1]
    portion = lax.all_gather(normed, "tp", axis=1, tiled=True)
    query_part = jnp.einsum("ocd,dk->ock", portion, w_query, preferred_element_type=jnp.float32)
    pair_part = jnp.einsum("ocd,dk->ock", portion, w_keyval, preferred_element_type=jnp.float32)
    projected = jnp.concatenate([query_part, pair_part], axis=-1)
    holding = projected.shape[0]
    length = projected.shape[1]
    head_width = HEAD_DIM
    positions = starts[:, None] + jnp.arange(length, dtype=jnp.int32)[None, :]
    queries = rotate(
        projected[..., :query_width].reshape(
            holding, length, query_width // head_width, head_width
        ),
        positions,
    ).astype(jnp.bfloat16)
    pair_piece = projected[..., query_width:].astype(jnp.bfloat16)
    sharers = tensor_size // KV_HEADS
    levels = sharers.bit_length() - 1
    sharer_rank = tensor_rank % sharers
    page_piece = stretch_pages
    for level_bit in range(levels):
        their_pairs, their_pages = from_partner((pair_piece, page_piece), "tp", level_bit)
        upper_half = tensor_rank // (1 << level_bit) % 2 == 1
        pair_piece = jnp.where(
            upper_half,
            jnp.concatenate([their_pairs, pair_piece], axis=-1),
            jnp.concatenate([pair_piece, their_pairs], axis=-1),
        )
        page_piece = jnp.where(
            upper_half,
            jnp.concatenate([their_pages, page_piece], axis=2),
            jnp.concatenate([page_piece, their_pages], axis=2),
        )
    live_mask = jnp.arange(length, dtype=jnp.int32)[None, :] < counts[:, None]
    rotated_keys = rotate(
        pair_piece[..., :head_width].astype(jnp.float32)[:, :, None, :], positions
    )[:, :, 0, :]
    head_pairs = (
        jnp.concatenate([rotated_keys, pair_piece[..., head_width:].astype(jnp.float32)], axis=-1)
        * live_mask[..., None].astype(jnp.float32)
    ).astype(jnp.bfloat16)
    piece_width = 2 * head_width // sharers
    columns = lax.dynamic_slice_in_dim(head_pairs, sharer_rank * piece_width, piece_width, 2)
    prefix = page_piece.reshape(holding, -1, 2 * head_width)
    attended = attend(queries, head_pairs, prefix, starts, counts)
    partial_value = jnp.einsum(
        "ock,kd->ocd",
        attended.reshape(holding, length, -1),
        w_out,
        preferred_element_type=jnp.float32,
    )
    summed = lax.psum_scatter(
        partial_value.astype(jnp.bfloat16), "tp", scatter_dimension=1, tiled=True
    ).astype(jnp.float32)
    share_rows = summed.shape[1]
    row_ids = tensor_rank * share_rows + jnp.arange(share_rows, dtype=jnp.int32)
    keep_rows = row_ids[None, :] < counts[:, None]
    result = jnp.where(keep_rows[..., None], summed, jnp.zeros_like(summed)).astype(jnp.bfloat16)
    return (result, columns)


def per_device(
    hidden, norm_gain, w_query, w_keyval, w_out, kv_cache, page_table, prefix_len, live_rows, plan
):
    groups = lax.axis_size("dp")
    holding = hidden.shape[0]
    slot_ids = jnp.arange(holding, dtype=jnp.int32)
    gathered_pages = kv_cache[page_table]
    target = jnp.arange(groups, dtype=jnp.int32)
    matches = plan[None, :] == target[:, None]
    present = jnp.any(matches, axis=1)
    chosen = jnp.argmax(matches, axis=1)
    labels = jnp.where(present, chosen, -1)
    local_rows, new_kv = layer(
        hidden, gathered_pages, prefix_len, live_rows, norm_gain, w_query, w_keyval, w_out
    )
    outgoing = jnp.where(
        present[:, None, None], local_rows[chosen], jnp.zeros((), local_rows.dtype)
    )
    arrived, labels_arrived = (
        lax.all_to_all(outgoing, "dp", split_axis=0, concat_axis=0, tiled=True),
        lax.all_to_all(labels, "dp", split_axis=0, concat_axis=0, tiled=True),
    )
    source = jnp.argmax(labels_arrived[None, :] == slot_ids[:, None], axis=1)
    result = arrived[source]
    return (result, new_kv)


def solution(mesh):
    in_specs = (
        P(("parts", "dp"), "tp", None),
        P(),
        P(None, "tp"),
        P(None, "tp"),
        P("tp", None),
        P(("parts", "dp"), "tp", None, None),
        P(("parts", "dp"), None),
        P(("parts", "dp")),
        P(("parts", "dp")),
        P(("parts", "dp")),
    )
    out_specs = (P(("parts", "dp"), "tp", None), P(("parts", "dp"), None, "tp"))
    return jax.shard_map(
        per_device, mesh=mesh, in_specs=in_specs, out_specs=out_specs, check_vma=False
    )
```

profile of v0, /device:TPU:0, one launch (start us, length us, event | category | flops | bytes accessed | tf_op | source)
XLA Modules:
  0.0 505.7 jit_solution(17708715125677177234)
XLA Ops:
  7.2 0.9 convert_element_type.69
  8.1 2.1 fusion.31
  10.2 1.9 fusion.33
  12.2 0.6 copy-done.1
  12.9 10.3 %gather_fusion = bf16[128,4,32,256]{3,2,1,0:T(8,128)(2,1)} fusion(bf16[128,4,32,256]{3,2,1,0:T(8,128)(2,1)} %param.21, s32[1024]{0:T(1024)S(1)} %pad_clamp_fusion.2), kind=kCustom, calls=%fused_computation | custom fusion | bytes 16777728 | tf_op jit(solution)/shard_map/gather | solution.py:194
  23.3 1.0 multiply_cosine_fusion
  24.3 140.3 %all-gather.2.cloned.1.call-done = bf16[4,128,8192]{2,1,0:T(8,128)(2,1)} async-done(((bf16[4,32,8192]{2,1,0:T(8,128)(2,1)}), bf16[4,128,8192]{2,1,0:T(8,128)(2,1)}) %all-gather.2.cloned.1.call-update) | async-done | bytes 8388624 | tf_op jit(solution)/shard_map/all_gather | solution.py:128
  164.6 14.3 %fusion.26 = f32[4,128,1024]{2,1,0:T(8,128)S(1)} fusion(bf16[4,128,8192]{2,1,0:T(8,128)(2,1)} %all-gather.2.cloned.1.call-done, bf16[8192,1024]{1,0:T(8,128)(2,1)} %param.18), kind=kOutput, calls=%fused_computation.50 | convolution fusion | flops 8589934592 | bytes 27262976 | tf_op jit(solution)/shard_map/ocd,dk->ock/dot_general | solution.py:129
  179.4 0.7 fusion.50
  180.1 1.0 copy-done.5
  181.1 2.6 copy-done.4
  183.7 2.3 fusion.36
  186.1 1.2 fusion.44
  187.3 0.8 subtract_convert_fusion
  188.1 1.6 pad_maximum_fusion
  189.8 0.8 fusion.39
  190.7 45.3 %while.88 = (s32[]{:T(128)}, bf16[4,128,8,128]{1,3,2,0:T(8,128)(2,1)}, bf16[4,128,256]{2,1,0:T(8,128)(2,1)}, s32[4]{0:T(128)S(1)}, bf16[4,128,8,128]{3,1,2,0:T(8...) while((s32[]{:T(128)}, ...), condition=%wide.region_11.12_spmd, body=%wide.region_2.11_spmd.sunk | while | flops 477399168 | bytes 14341821 | solution.py:115
  191.8 1.0 dynamic-slice_bitcast_fusion.15
  192.8 0.9 dynamic-slice_bitcast_fusion.16
  193.6 0.6 dynamic_slice.72
  194.2 0.6 iota_compare_fusion.6
  195.3 1.7 dynamic-slice_bitcast_fusion.17
  197.0 3.2 while.89
  200.5 3.1 while.90
  201.1 0.9 fusion.70
  202.7 0.9 fusion.70
  203.6 0.7 bitcast_dynamic-update-slice_fusion.2
  205.5 1.0 dynamic-slice_bitcast_fusion.15
  206.5 0.9 dynamic-slice_bitcast_fusion.16
  207.3 0.6 dynamic_slice.72
  207.9 0.6 iota_compare_fusion.6
  209.0 1.7 dynamic-slice_bitcast_fusion.17
  210.7 3.2 while.89
  214.2 3.1 while.90
  214.8 0.9 fusion.70
  216.3 0.9 fusion.70
  217.3 0.7 bitcast_dynamic-update-slice_fusion.2
  219.2 1.0 dynamic-slice_bitcast_fusion.15
  220.1 0.9 dynamic-slice_bitcast_fusion.16
  221.0 0.6 dynamic_slice.72
  221.6 0.6 iota_compare_fusion.6
  222.6 1.7 dynamic-slice_bitcast_fusion.17
  224.4 1.6 while.89
  226.3 1.5 while.90
  226.9 0.9 fusion.70
  227.8 0.8 bitcast_dynamic-update-slice_fusion.2
  229.7 1.0 dynamic-slice_bitcast_fusion.15
  230.7 0.9 dynamic-slice_bitcast_fusion.16
  232.1 0.6 iota_compare_fusion.6
  233.2 1.7 dynamic-slice_bitcast_fusion.17
  235.2 0.8 bitcast_dynamic-update-slice_fusion.2
  236.0 14.8 %fusion.28 = bf16[4,128,8192]{2,1,0:T(8,128)(2,1)} fusion(bf16[4,128,1024]{1,2,0:T(8,128)(2,1)} %bitcast.136, bf16[1024,8192]{1,0:T(8,128)(2,1)} %param.20), kind=kOutput, calls=%fused_computation.52 | convolution fusion | flops 8594128896 | bytes 26214400 | tf_op jit(solution)/shard_map/ock,kd->ocd/dot_general | solution.py:172
  250.8 0.6 copy-done.6
  251.6 0.6 iota_reduce_fusion.1
  252.2 0.7 copy.50
  252.9 70.4 %all-to-all-start.1 = ((s32[4,1,1]{2,1,0:T(1,128)}), s32[4,1,1]{2,1,0:T(1,128)S(1)}, u32[]{:S(2)}, u32[]{:S(2)}) async-start(s32[4,1,1]{2,1,0:T(1,128)} %copy.50), calls=%async_computation.2 | async-start | bytes 4096 | tf_op jit(solution)/shard_map/all_to_all | solution.py:208
  323.3 137.1 %reduce-scatter.2.cloned.1.call-done = bf16[4,32,8192]{2,1,0:T(8,128)(2,1)} async-done(((bf16[4,128,8192]{2,1,0:T(8,128)(2,1)}), bf16[4,32,8192]{2,1,0:T(8,128)(2,1)}) %reduce-scatter.2.cloned.1.call-update) | async-done | bytes 2097168 | tf_op jit(solution)/shard_map/reduce_scatter | solution.py:178
  460.5 2.1 select_convert_fusion
  462.5 2.0 gather_fusion.1
  464.5 3.1 broadcast_select_fusion
  467.6 3.6 all-to-all-start
  471.4 0.7 iota_reduce_fusion
  472.2 24.7 %all-to-all-done = bf16[4,32,8192]{2,1,0:T(8,128)(2,1)S(1)} async-done(((bf16[4,32,8192]{2,1,0:T(8,128)(2,1)}), bf16[4,32,8192]{2,1,0:T(8,128)(2,1)S(1)}, u32[]{:S(2)}, u32[]{:S(2)}) %all-to-all-start) | async-done | bytes 2097184 | tf_op jit(solution)/shard_map/all_to_all | solution.py:207
  496.9 2.0 gather_fusion.2
  (92 shorter events, 17.5 us)
Async XLA Ops:
  7.2 3.0 copy-start
  7.2 157.4 %all-gather.2.cloned.1.call-start = ((), (), s32[]{:S(2)}) async-start(), calls=%async_computation.3 | async-start | bytes 10485760 | tf_op jit(solution)/shard_map/all_gather | solution.py:128
  12.1 0.7 copy-start.1
  12.1 448.3 %reduce-scatter.2.cloned.1.call-start = ((), (), s32[]{:S(2)}) async-start(), calls=%async_computation.4 | async-start | bytes 10485760 | tf_op jit(solution)/shard_map/reduce_scatter | solution.py:178
  12.9 10.3 %copy-start.2 = (s32[4]{0:T(128)S(1)}, s32[4]{0:T(128)}, u32[]{:S(2)}) copy-start(s32[4]{0:T(128)} %param.23) | copy-start | bytes 52
  12.9 10.4 %copy-start.3 = (s32[4]{0:T(128)S(1)}, s32[4]{0:T(128)}, u32[]{:S(2)}) copy-start(s32[4]{0:T(128)} %param.24) | copy-start | bytes 52
  178.9 2.2 copy-start.5
  179.4 4.3 copy-start.4
  250.8 0.7 copy-start.6
  252.9 214.8 %all-to-all-start.1 = ((s32[4,1,1]{2,1,0:T(1,128)}), s32[4,1,1]{2,1,0:T(1,128)S(1)}, u32[]{:S(2)}, u32[]{:S(2)}) async-start(s32[4,1,1]{2,1,0:T(1,128)} %copy.50), calls=%async_computation.2 | async-start | bytes 4096 | tf_op jit(solution)/shard_map/all_to_all | solution.py:208
  467.6 29.3 %all-to-all-start = ((bf16[4,32,8192]{2,1,0:T(8,128)(2,1)}), bf16[4,32,8192]{2,1,0:T(8,128)(2,1)S(1)}, u32[]{:S(2)}, u32[]{:S(2)}) async-start(bf16[4,32,8192]{2,1,0:T(8,128)(2,1)} %broadcast_select_fusion), calls=%async_computation.1 | async-start | bytes 4194304 | tf_op jit(solution)/shard_map/all_to_all | solution.py:207
Sparse Core Ops, SparseCore 0:
  12.3 152.3 all-gather.1
  250.9 209.4 reduce-scatter.1
where the time goes:
time: 507 us; the launch traced here: 506 us
  waiting for transfers between devices  302 us (60%)
  starting transfers between devices  74.1 us (15%)
  matrix products  40.3 us (8%)
  local copies, waits for them, and re-layouts  39.8 us (8%)
  other arithmetic  32 us (6%)
  between operations  14.2 us (3%)
    all_gather x1, waiting for transfers between devices, layer(): portion = lax.all_gather(normed, 'tp', axis=1, tiled=True)  140 us
    reduce_scatter x1, waiting for transfers between devices, layer(): lax.psum_scatter(partial_value.astype(jnp.bfloat16), 'tp', scatter_dimens...  137 us
    all_to_all x1, starting transfers between devices, per_device(): lax.all_to_all(labels, 'dp', split_axis=0, concat_axis=0, tiled=True)  70.4 us
    all_to_all x1, waiting for transfers between devices, per_device(): lax.all_to_all(outgoing, 'dp', split_axis=0, concat_axis=0, tiled=True)  24.7 us
    dot_general x1, matrix products, layer(): jnp.einsum('ock,kd->ocd', attended.reshape(holding, length, -1), w_out, p...  14.8 us
    dot_general x1, matrix products, layer(): jnp.einsum('ocd,dk->ock', portion, w_query, preferred_element_type=jnp.fl...  14.3 us
    squeeze x12, local copies, waits for them, and re-layouts, attend(): return lax.map(attend_one, (queries, head_pairs, prefix, starts, counts))  14.2 us
    gather x1, local copies, waits for them, and re-layouts, per_device(): gathered_pages = kv_cache[page_table]  10.3 us
  transfers between devices with their start and end apart: 4, of which 3 were waited for; matrix products, arithmetic and copies ran while one was open for 4% of the time, Pallas kernels for 0%

commit v1 on v0

--- a/solution.py
+++ b/solution.py
@@ -1,9 +1,13 @@
+import functools
 import math
 
 import jax
 import jax.numpy as jnp
 from jax import lax
+from jax.experimental import pallas as pl
+from jax.experimental.pallas import tpu as pltpu
 from jax.sharding import PartitionSpec as P
+
 
 KV_HEADS = 4
 HEAD_DIM = 128
@@ -14,6 +18,8 @@
 EPSILON = 1e-05
 ROPE_BASE = 500000.0
 MASKED = -1e30
+HBM = pl.BlockSpec(memory_space=pl.ANY)
+GRANT = 20 << 20
 
 
 def from_partner(value, axis, distance):
@@ -77,7 +83,7 @@
 
     def first_pass(block_id, state_pair):
         old_max, old_sum = state_pair
-        scores, key_block = block_scores(block_id)
+        scores, _ = block_scores(block_id)
         raised_max = jnp.maximum(old_max, jnp.max(scores, axis=-1))
         new_sum = old_sum * jnp.exp(old_max - raised_max) + jnp.sum(
             jnp.exp(scores - raised_max[..., None]), axis=-1
@@ -185,7 +191,7 @@
     return (result, columns)
 
 
-def per_device(
+def general(
     hidden, norm_gain, w_query, w_keyval, w_out, kv_cache, page_table, prefix_len, live_rows, plan
 ):
     groups = lax.axis_size("dp")
@@ -212,6 +218,532 @@
     return (result, new_kv)
 
 
+LINE = 4
+
+
+def pick_of(info_ref, turn, holding):
+    target = info_ref[1] ^ turn
+    pick = 0
+    for place in range(1, holding):
+        pick = jnp.where(info_ref[2 + place] == target, place, pick)
+    return pick
+
+
+def norm_kernel(info_ref, hidden_ref, gain_ref, *out_refs):
+    step = pl.program_id(0)
+    widened = hidden_ref[0].astype(jnp.float32)
+    mean = jnp.mean(widened * widened, axis=-1, keepdims=True)
+    gain = gain_ref[...].astype(jnp.float32)[None, :]
+    normed = (widened * lax.rsqrt(mean + EPSILON) * gain).astype(jnp.bfloat16)
+    for place, out_ref in enumerate(out_refs):
+        @pl.when(step == place)
+        def _():
+            out_ref[...] = normed
+
+
+def norm_some(info, turns, hidden, gain):
+    holding, rows, width = hidden.shape
+
+    def chosen(i, info_ref):
+        turn = jnp.int32(turns[0])
+        for place in range(1, len(turns)):
+            turn = jnp.where(i == place, turns[place], turn)
+        return (pick_of(info_ref, turn, holding), 0, 0)
+
+    return pl.pallas_call(
+        norm_kernel,
+        grid_spec=pltpu.PrefetchScalarGridSpec(
+            num_scalar_prefetch=1,
+            grid=(len(turns),),
+            in_specs=[
+                pl.BlockSpec((1, rows, width), chosen),
+                pl.BlockSpec((width,), lambda i, info_ref: (0,)),
+            ],
+            out_specs=[pl.BlockSpec((rows, width), lambda i, info_ref: (0, 0))] * len(turns),
+        ),
+        out_shape=[jax.ShapeDtypeStruct((rows, width), jnp.bfloat16)] * len(turns),
+        compiler_params=pltpu.CompilerParams(vmem_limit_bytes=GRANT),
+        cost_estimate=pl.CostEstimate(
+            flops=4 * rows * width * len(turns),
+            bytes_accessed=4 * rows * width * len(turns),
+            transcendentals=rows,
+        ),
+        name="norm_some",
+    )(info, hidden, gain)
+
+
+def load_kernel(count, *refs):
+    sources, kept, sems = refs[:count], refs[-1 - count : -1], refs[-1]
+    copies = [
+        pltpu.make_async_copy(sources[place], kept[place], sems.at[place]) for place in range(count)
+    ]
+    for item in copies:
+        item.start()
+    for item in copies:
+        item.wait()
+
+
+def load(*arrays, after=()):
+    kept = pl.BlockSpec(memory_space=pltpu.MemorySpace.VMEM)
+    return pl.pallas_call(
+        functools.partial(load_kernel, len(arrays)),
+        in_specs=[HBM] * (len(arrays) + len(after)),
+        out_specs=[kept] * len(arrays),
+        out_shape=[pltpu.VMEM(item.shape, item.dtype) for item in arrays],
+        scratch_shapes=[pltpu.SemaphoreType.DMA((len(arrays),))],
+        compiler_params=pltpu.CompilerParams(vmem_limit_bytes=GRANT),
+        name="load",
+    )(*stored_of(*arrays), *after)
+
+
+def stored_of(*arrays):
+    return [pltpu.with_memory_space_constraint(item, pltpu.MemorySpace.HBM) for item in arrays]
+
+
+def resident_of(*arrays):
+    return [pltpu.with_memory_space_constraint(item, pltpu.MemorySpace.VMEM) for item in arrays]
+
+
+def project_kernel(count, share, places, turn, holding, head_width, tile, aliased, info_ref, *refs):
+    sources = refs[:count]
+    query_ref, pair_ref, cosine_ref, sine_ref = refs[count : count + 4]
+    refs = refs[count + 4 + aliased :]
+    turned_ref, kept_ref, placed_ref = refs[:3]
+    rows_ref, sems = refs[3:]
+    wide = query_ref.shape[1]
+    rank = info_ref[0]
+    live = info_ref[2 + 2 * holding + pick_of(info_ref, turn, holding)]
+
+    def copy(place):
+        source, half = places[place][:2]
+        start = pl.multiple_of(places[place][2](rank), share)
+        return pltpu.make_async_copy(
+            sources[source].at[pl.ds(half * share, share)],
+            rows_ref.at[pl.ds(start, share)],
+            sems.at[place],
+        )
+
+    for place in range(len(places)):
+        @pl.when(places[place][3](rank))
+        def _():
+            copy(place).start()
+    for place in range(len(places)):
+        @pl.when(places[place][3](rank))
+        def _():
+            copy(place).wait()
+
+    length = rows_ref.shape[0]
+    cosine = cosine_ref[0]
+    sine = sine_ref[0]
+    half = head_width // 2
+
+    def turn_rows(values):
+        return values * cosine + pltpu.roll(values, half, 1) * sine
+
+    @pl.loop(0, wide // tile)
+    def _(step):
+        span = pl.ds(pl.multiple_of(step * tile, tile), tile)
+        part = jnp.dot(rows_ref[...], query_ref[:, span], preferred_element_type=jnp.float32)
+        for head in range(tile // head_width):
+            turned = turn_rows(part[:, head * head_width : (head + 1) * head_width])
+            place = pl.ds(pl.multiple_of((step * (tile // head_width) + head) * length, length), length)
+            turned_ref[:, place] = turned.T.astype(turned_ref.dtype)
+
+    pairs = jnp.dot(rows_ref[...], pair_ref[...], preferred_element_type=jnp.float32)
+    pairs = pairs.astype(jnp.bfloat16).astype(jnp.float32)
+    keys, values = pairs[:, :head_width], pairs[:, head_width:]
+    row = lax.broadcasted_iota(jnp.int32, keys.shape, 0)
+    keys = jnp.where(row < live, turn_rows(keys), 0.0).astype(kept_ref.dtype)
+    values = jnp.where(row < live, values, 0.0).astype(kept_ref.dtype)
+    for target in (kept_ref, placed_ref.at[0]):
+        target[:, :head_width] = keys
+        target[:, head_width:] = values
+
+
+def project(info, turn, sources, places, w_query, w_keyval, cosine, sine, placed):
+    share = sources[0].shape[0]
+    width, wide = w_query.shape
+    narrow = w_keyval.shape[1]
+    holding, length, head_width = cosine.shape
+    tile = min(wide, 2 * head_width)
+    resident = pl.BlockSpec(memory_space=pltpu.MemorySpace.VMEM)
+    picked = lambda i, info_ref: (pick_of(info_ref, turn, holding), 0, 0)
+    fixed = lambda i, info_ref: (0, 0)
+    lanes = wide // head_width * length
+    extra = [] if placed is None else [placed]
+    return pl.pallas_call(
+        functools.partial(
+            project_kernel, len(sources), share, places, turn, holding, head_width, tile, len(extra)
+        ),
+        grid_spec=pltpu.PrefetchScalarGridSpec(
+            num_scalar_prefetch=1,
+            grid=(1,),
+            in_specs=[HBM] * len(sources)
+            + [resident] * 2
+            + [pl.BlockSpec((1, length, head_width), picked)] * 2
+            + [HBM] * len(extra),
+            out_specs=[
+                pl.BlockSpec((head_width, lanes), fixed),
+                pl.BlockSpec((length, narrow), fixed),
+                pl.BlockSpec((1, length, narrow), picked),
+            ],
+            scratch_shapes=[
+                pltpu.VMEM((length, width), jnp.bfloat16),
+                pltpu.SemaphoreType.DMA((len(places),)),
+            ],
+        ),
+        out_shape=[
+            jax.ShapeDtypeStruct((head_width, lanes), jnp.bfloat16),
+            jax.ShapeDtypeStruct((length, narrow), jnp.bfloat16),
+            jax.ShapeDtypeStruct((holding, length, narrow), jnp.bfloat16),
+        ],
+        input_output_aliases={len(sources) + 5: 2} if extra else {},
+        compiler_params=pltpu.CompilerParams(vmem_limit_bytes=GRANT),
+        cost_estimate=pl.CostEstimate(
+            flops=2 * length * width * (wide + narrow),
+            bytes_accessed=2 * length * width,
+            transcendentals=0,
+        ),
+        name="project",
+    )(info, *stored_of(*sources), *resident_of(w_query, w_keyval), cosine, sine, *extra)
+
+
+def stretch_kernel(
+    count, part, pieces, turn, holding, limit, length, group, tile, info_ref, turned_ref, kept_ref, cache_ref, out_w_ref, *refs
+):
+    outs = refs[:count]
+    stored, product, heads_ref, top_ref, sum_ref, acc_ref, page_sems, out_sems = refs[count:]
+    block = cache_ref.shape[1]
+    head_width = kept_ref.shape[1] // 2
+    lanes = turned_ref.shape[1]
+    rank = info_ref[0]
+    pick = pick_of(info_ref, turn, holding)
+    pages = info_ref[2 + holding + pick] // block
+    live = info_ref[2 + 2 * holding + pick]
+    base = 2 + 3 * holding + pick * limit
+    tiles = product.shape[0]
+    scale = (1.0 / math.sqrt(head_width)) * math.log2(math.e)
+
+    def page_copy(place):
+        start = pl.multiple_of(place * block, block)
+        return pltpu.make_async_copy(
+            cache_ref.at[info_ref[base + place]], stored.at[pl.ds(start, block)], page_sems.at[place]
+        )
+
+    @pl.loop(0, pages)
+    def _(place):
+        page_copy(place).start()
+
+    def fold(keys, values, mask):
+        scores = jnp.dot(keys, turned_ref[...], preferred_element_type=jnp.float32)
+        if mask is not None:
+            scores = jnp.where(mask, scores, MASKED)
+            top = jnp.max(scores, axis=0, keepdims=True)
+        else:
+            top = jnp.maximum(top_ref[...], jnp.max(scores, axis=0, keepdims=True))
+        exps = jnp.exp2((scores - top) * scale)
+        summed = jnp.sum(exps, axis=0, keepdims=True)
+        taken = lax.dot_general(
+            values, exps.astype(jnp.bfloat16), (((0,), (0,)), ((), ())), preferred_element_type=jnp.float32
+        )
+        if mask is not None:
+            sum_ref[...] = summed
+            acc_ref[...] = taken
+        else:
+            fade = jnp.exp2((top_ref[...] - top) * scale)
+            sum_ref[...] = sum_ref[...] * fade + summed
+            acc_ref[...] = acc_ref[...] * fade + taken
+        top_ref[...] = top
+
+    key_row = lax.broadcasted_iota(jnp.int32, (length, lanes), 0)
+    query_row = lax.rem(lax.broadcasted_iota(jnp.int32, (length, lanes), 1), length)
+    fold(kept_ref[:, :head_width], kept_ref[:, head_width:], (key_row <= query_row) & (key_row < live))
+
+    def fold_span(first, span):
+        for item in range(span):
+            page_copy(first + item).wait()
+        rows = pl.ds(pl.multiple_of(first * block, block), span * block)
+        fold(stored[rows, :head_width], stored[rows, head_width:], None)
+
+    whole = pages // group
+
+    @pl.loop(0, whole)
+    def _(step):
+        fold_span(step * group, group)
+
+    @pl.loop(whole * group, pages)
+    def _(place):
+        fold_span(place, 1)
+
+    share = acc_ref[...] / sum_ref[...]
+    row = lax.broadcasted_iota(jnp.int32, (length, head_width), 0)
+    for head in range(lanes // length):
+        span = slice(head * length, (head + 1) * length)
+        heads_ref[:, head * head_width : (head + 1) * head_width] = jnp.where(
+            row < live, share[:, span].T, 0.0
+        ).astype(heads_ref.dtype)
+
+    def out_copies(place):
+        copies = []
+        for item, (out, half, row_start) in enumerate(pieces):
+            start = pl.multiple_of(row_start(rank), part)
+            columns = pl.ds(pl.multiple_of(place * tile, tile), tile)
+            copies.append(
+                pltpu.make_async_copy(
+                    product.at[place, pl.ds(start, part)],
+                    outs[out].at[pl.ds(half * part, part), columns],
+                    out_sems.at[item, place],
+                )
+            )
+        return copies
+
+    @pl.loop(0, tiles)
+    def _(place):
+        columns = pl.ds(pl.multiple_of(place * tile, tile), tile)
+        product[place] = jnp.dot(
+            heads_ref[...], out_w_ref[:, columns], preferred_element_type=jnp.float32
+        ).astype(product.dtype)
+        for item in out_copies(place):
+            item.start()
+
+    @pl.loop(0, tiles)
+    def _(place):
+        for item in out_copies(place):
+            item.wait()
+
+
+def attend_stretch(info, turn, turned, kept, cache, w_out, sizes, pieces, part, holding, limit, length):
+    head_width, lanes = turned.shape
+    block = cache.shape[1]
+    inner, width = w_out.shape
+    tile = min(width, 1024)
+    tiles = width // tile
+    group = min(4, limit)
+    return pl.pallas_call(
+        functools.partial(
+            stretch_kernel, len(sizes), part, pieces, turn, holding, limit, length, group, tile
+        ),
+        grid_spec=pltpu.PrefetchScalarGridSpec(
+            num_scalar_prefetch=1,
+            grid=(1,),
+            in_specs=[
+                pl.BlockSpec(turned.shape, lambda i, info_ref: (0, 0)),
+                pl.BlockSpec(kept.shape, lambda i, info_ref: (0, 0)),
+                HBM,
+                pl.BlockSpec(memory_space=pltpu.MemorySpace.VMEM),
+            ],
+            out_specs=[HBM] * len(sizes),
+            scratch_shapes=[
+                pltpu.VMEM((limit * block, 2 * head_width), jnp.bfloat16),
+                pltpu.VMEM((tiles, length, tile), jnp.bfloat16),
+                pltpu.VMEM((length, inner), jnp.bfloat16),
+                pltpu.VMEM((1, lanes), jnp.float32),
+                pltpu.VMEM((1, lanes), jnp.float32),
+                pltpu.VMEM((head_width, lanes), jnp.float32),
+                pltpu.SemaphoreType.DMA((limit,)),
+                pltpu.SemaphoreType.DMA((len(pieces), tiles)),
+            ],
+        ),
+        out_shape=[jax.ShapeDtypeStruct((size, width), jnp.bfloat16) for size in sizes],
+        compiler_params=pltpu.CompilerParams(vmem_limit_bytes=GRANT),
+        cost_estimate=pl.CostEstimate(
+            flops=4 * lanes * head_width * limit * block + 2 * length * inner * width,
+            bytes_accessed=4 * limit * block * head_width,
+            transcendentals=lanes * limit * block,
+        ),
+        name="attend",
+    )(info, turned, kept, *stored_of(cache), *resident_of(w_out))
+
+
+def finish_kernel(turns, info_ref, labels_ref, *refs):
+    count = len(turns) - 1
+    moved_refs, terms = refs[:count], refs[count:-4]
+    out_ref, last_ref, sems, last_sem = refs[-4:]
+    group = info_ref[1]
+
+    def copy(place):
+        return pltpu.make_async_copy(
+            moved_refs[place], out_ref.at[labels_ref[group ^ turns[place]]], sems.at[place]
+        )
+
+    for place in range(count):
+        copy(place).start()
+    total = terms[0][...].astype(jnp.float32)
+    for term in terms[1:]:
+        total += term[...].astype(jnp.float32)
+    last_ref[...] = total.astype(last_ref.dtype)
+    last = pltpu.make_async_copy(last_ref, out_ref.at[labels_ref[group ^ turns[count]]], last_sem)
+    last.start()
+    for place in range(count):
+        copy(place).wait()
+    last.wait()
+
+
+def finish(info, labels, turns, arrived, terms):
+    rows, width = terms[0].shape
+    whole = pl.BlockSpec((rows, width), lambda i, *_: (0, 0))
+    return pl.pallas_call(
+        functools.partial(finish_kernel, turns),
+        grid_spec=pltpu.PrefetchScalarGridSpec(
+            num_scalar_prefetch=2,
+            grid=(1,),
+            in_specs=[whole] * (len(arrived) + len(terms)),
+            out_specs=HBM,
+            scratch_shapes=[
+                pltpu.VMEM((rows, width), jnp.bfloat16),
+                pltpu.SemaphoreType.DMA((len(arrived),)),
+                pltpu.SemaphoreType.DMA,
+            ],
+        ),
+        out_shape=jax.ShapeDtypeStruct((len(turns), rows, width), jnp.bfloat16),
+        compiler_params=pltpu.CompilerParams(vmem_limit_bytes=GRANT),
+        cost_estimate=pl.CostEstimate(
+            flops=rows * width * len(terms), bytes_accessed=22 * rows * width, transcendentals=0
+        ),
+        name="finish",
+    )(info, labels, *arrived, *terms)
+
+
+def position_tables(starts, length):
+    half = HEAD_DIM // 2
+    frequency = ROPE_BASE ** (-jnp.arange(half, dtype=jnp.float32) / half)
+    positions = starts[:, None] + jnp.arange(length, dtype=jnp.int32)[None, :]
+    angles = positions.astype(jnp.float32)[..., None] * frequency
+    cosine = jnp.cos(angles)
+    sine = jnp.sin(angles)
+    return (
+        jnp.concatenate([cosine, cosine], axis=-1),
+        jnp.concatenate([-sine, sine], axis=-1),
+    )
+
+
+def added(*terms):
+    total = functools.reduce(lambda a, b: a + b, [term.astype(jnp.float32) for term in terms])
+    return total.astype(jnp.bfloat16)
+
+
+def paired(
+    hidden, norm_gain, w_query, w_keyval, w_out, kv_cache, page_table, prefix_len, live_rows, plan
+):
+    groups = lax.axis_size("dp")
+    group = lax.axis_index("dp")
+    rank = lax.axis_index("tp")
+    holding, share, _ = hidden.shape
+    length = share * lax.axis_size("tp")
+    limit = page_table.shape[1]
+    cache = kv_cache.reshape(kv_cache.shape[0], -1, kv_cache.shape[-1])
+    slot_ids = jnp.arange(holding, dtype=jnp.int32)
+    info = jnp.concatenate(
+        [jnp.stack([rank, group]), plan, prefix_len, live_rows, page_table.reshape(-1)]
+    ).astype(jnp.int32)
+    turns = list(range(groups))[::-1]
+    steps = len(turns)
+    sides = [(0, 1), (1, 0), (2, 3), (3, 2)]
+    middle = [(1, 2), (2, 1)]
+    outward = [(1, 0), (2, 3)]
+    inward = [(0, 1), (3, 2)]
+    is_inner = lambda r: (r == 1) | (r == 2)
+    is_outer = lambda r: (r == 0) | (r == 3)
+    always = lambda r: r >= 0
+    block = lambda distance: lambda r: (r ^ distance) * share
+    nearer = lambda r: jnp.where(is_inner(r), r ^ 3, r ^ 2) * share
+    farther = lambda r: jnp.where(is_inner(r), r ^ 2, r ^ 3) * share
+
+    (first,) = norm_some(info, turns[:1], hidden, norm_gain)
+    normed = [first, *norm_some(info, turns[1:], hidden, norm_gain)]
+    matches = plan[None, :] == jnp.arange(groups, dtype=jnp.int32)[:, None]
+    chosen = jnp.sum(jnp.where(matches, slot_ids[None, :], 0), axis=1)
+    labels = lax.all_to_all(chosen, "dp", split_axis=0, concat_axis=0, tiled=True)
+    cosine, sine = position_tables(prefix_len, length)
+    w_query, w_keyval = load(w_query, w_keyval, after=(labels,))
+    (w_out,) = load(w_out)
+
+    sources = []
+    for step in range(steps):
+        own = normed[step]
+        sibling = lax.ppermute(own, "tp", sides)
+        if step == 0:
+            first_in = lax.ppermute(own, "tp", middle)
+            second_in = lax.ppermute(sibling, "tp", middle)
+            first_out = lax.ppermute(first_in, "tp", outward)
+            second_out = lax.ppermute(second_in, "tp", outward)
+            sources.append(
+                (
+                    [own, sibling, first_in, second_in, first_out, second_out],
+                    [
+                        (0, 0, block(0), always),
+                        (1, 0, block(1), always),
+                        (2, 0, block(3), is_inner),
+                        (3, 0, block(2), is_inner),
+                        (4, 0, block(2), is_outer),
+                        (5, 0, block(3), is_outer),
+                    ],
+                )
+            )
+        else:
+            pair = jnp.concatenate([own, sibling], axis=0)
+            crossed = lax.ppermute(pair, "tp", middle)
+            passed = lax.ppermute(crossed, "tp", outward)
+            sources.append(
+                (
+                    [own, sibling, crossed, passed],
+                    [
+                        (0, 0, block(0), always),
+                        (1, 0, block(1), always),
+                        (2, 0, block(3), is_inner),
+                        (2, 1, block(2), is_inner),
+                        (3, 0, block(2), is_outer),
+                        (3, 1, block(3), is_outer),
+                    ],
+                )
+            )
+
+    placed = None
+    arrived = []
+    for step, turn in enumerate(turns):
+        values, places = sources[step]
+        turned, kept, placed = project(
+            info, turn, values, places, w_query, w_keyval, cosine, sine, placed
+        )
+        if step == steps - 1:
+            sizes, pieces = (share,) * 4, [(d, 0, block(d)) for d in range(4)]
+        else:
+            sizes = (2 * share, share, share)
+            pieces = [(0, 0, nearer), (0, 1, farther), (1, 0, block(1)), (2, 0, block(0))]
+        parts = attend_stretch(
+            info, turn, turned, kept, cache, w_out, sizes, pieces, share, holding, limit, length
+        )
+        if step == steps - 1:
+            own, beside, beyond, across = parts
+            one = lax.ppermute(across, "tp", inward)
+            two = lax.ppermute(beyond, "tp", inward)
+            three = lax.ppermute(beside, "tp", inward)
+            four = lax.ppermute(added(beyond, one), "tp", middle)
+            five = lax.ppermute(added(across, two), "tp", middle)
+            six = lax.ppermute(added(beside, four), "tp", outward)
+            result = finish(info, labels, turns, arrived, [own, three, five, six])
+        else:
+            far_part, beside, own = parts
+            joined = lax.ppermute(far_part, "tp", inward)
+            crossed = lax.ppermute(added(far_part, joined), "tp", middle)
+            swapped = lax.ppermute(added(beside, crossed[share:]), "tp", sides)
+            branch = added(own, crossed[:share], swapped)
+            pairs = [(g, g ^ turn) for g in range(groups)]
+            arrived.append(lax.ppermute(branch, "dp", pairs))
+    return (result, placed)
+
+
+def per_device(
+    hidden, norm_gain, w_query, w_keyval, w_out, kv_cache, page_table, prefix_len, live_rows, plan
+):
+    groups = lax.axis_size("dp")
+    even = groups == hidden.shape[0] == LINE
+    route = paired if even and lax.axis_size("tp") == KV_HEADS == LINE else general
+    return route(
+        hidden, norm_gain, w_query, w_keyval, w_out, kv_cache, page_table, prefix_len, live_rows, plan
+    )
+
+
 def solution(mesh):
     in_specs = (
         P(("parts", "dp"), "tp", None),

time: 507 us -> 341 us (0.67)
  waiting for transfers between devices: 302 us -> 144 us
  Pallas kernels: 0 us -> 80 us
  matrix products: 40.3 us -> 0 us
  other arithmetic: 32 us -> 8.25 us
  local copies, waits for them, and re-layouts: 39.8 us -> 17.1 us
  starting transfers between devices: 74.1 us -> 88.4 us
  between operations: 14.2 us -> 1.48 us
    ppermute x0 -> x32, waiting for transfers between devices: none -> 144 us  [the longest x3 47.7 us: paired(): joined = lax.ppermute(far_part, 'tp', inward)]
    all_gather x1 -> x0, waiting for transfers between devices: 140 us -> none  [layer(): portion = lax.all_gather(normed, 'tp', axis=1, tiled=True)]
    reduce_scatter x1 -> x0, waiting for transfers between devices: 137 us -> none  [layer(): lax.psum_scatter(partial_value.astype(jnp.bfloat16), 'tp', scatter_dimens...]
    ppermute x0 -> x32, starting transfers between devices: none -> 85.1 us  [the longest x3 29.7 us: paired(): swapped = lax.ppermute(added(beside, crossed[share:]), 'tp', sides)]
    pallas_call x0 -> x13, Pallas kernels: none -> 80 us  [the longest x4 32.1 us: attend_stretch(): pl.pallas_call(functools.partial(stretch_kernel, len(sizes), part, pieces...]
    all_to_all x2 -> x1, starting transfers between devices: 74 us -> 3.22 us  [paired(): lax.all_to_all(chosen, 'dp', split_axis=0, concat_axis=0, tiled=True)]
    dot_general x21 -> x0, matrix products: 40.3 us -> none  [the longest x1 14.8 us: layer(): jnp.einsum('ock,kd->ocd', attended.reshape(holding, length, -1), w_out, p...]
    all_to_all x2 -> x1, waiting for transfers between devices: 24.7 us -> 0.01 us  [paired(): lax.all_to_all(chosen, 'dp', split_axis=0, concat_axis=0, tiled=True)]
  transfers between devices with their start and end apart: 4 -> 33, of which waited for: 3 -> 12; matrix products, arithmetic and copies ran while one was open for 4% -> 3% of each run, Pallas kernels for 0% -> 22%
where the time goes in v1:
time: 341 us; the launch traced here: 340 us
  waiting for transfers between devices  144 us (42%)
  starting transfers between devices  88.4 us (26%)
  Pallas kernels  80 us (23%)
  local copies, waits for them, and re-layouts  17.1 us (5%)
  other arithmetic  8.25 us (2%)
    ppermute x3, waiting for transfers between devices, paired(): joined = lax.ppermute(far_part, 'tp', inward)  47.7 us
    ppermute x3, waiting for transfers between devices, paired(): swapped = lax.ppermute(added(beside, crossed[share:]), 'tp', sides)  36.6 us
    ppermute x4, waiting for transfers between devices, paired(): sibling = lax.ppermute(own, 'tp', sides)  32.6 us
    pallas_call x4, Pallas kernels, attend_stretch(): pl.pallas_call(functools.partial(stretch_kernel, len(sizes), part, pieces...  32.1 us
    pallas_call x4, Pallas kernels, project(): pl.pallas_call(functools.partial(project_kernel, len(sources), share, pla...  30.5 us
    ppermute x3, starting transfers between devices, paired(): swapped = lax.ppermute(added(beside, crossed[share:]), 'tp', sides)  29.7 us
    ppermute x3, starting transfers between devices, paired(): joined = lax.ppermute(far_part, 'tp', inward)  24.9 us
    unnamed x44, local copies, waits for them, and re-layouts  14.9 us
  transfers between devices with their start and end apart: 33, of which 12 were waited for; matrix products, arithmetic and copies ran while one was open for 3% of the time, Pallas kernels for 22%

profile of v1, /device:TPU:0, one launch (start us, length us, event | category | flops | bytes accessed | tf_op | source)
XLA Modules:
  0.0 339.6 jit_solution(7791174698051823709)
XLA Ops:
  0.6 0.8 reshape.41
  1.4 0.8 concatenate.18.info_ref
  2.2 1.6 copy-done.3
  3.8 0.7 copy-done.8
  4.5 1.7 norm_some.3
  6.2 3.1 collective-permute-start.9
  9.3 0.9 norm_some.2.refs_0_
  10.3 1.5 collective-permute-start.1
  11.8 4.1 %collective-permute-start.16 = (bf16[32,8192]{1,0:T(8,128)(2,1)S(1)}, bf16[32,8192]{1,0:T(8,128)(2,1)S(1)}, u32[]{:S(2)}, u32[]{:S(2)}) collective-permute-start(bf16[32,8192]{1,0:T(8,128)(2,1)S(1)} %get-tuple-element.46.refs_0_), channel_id=1, source_target_pairs={{0,1},{1,0},{2,3},{3,2},{4,5},{5,4},{6,7},{7,6},{8,9},{9,8},{10,11... | collective-permute-start | bytes 1572872 | tf_op jit(solution)/shard_map/ppermute | solution.py:664
  16.0 6.1 %collective-permute-done.9.refs_1_ = bf16[32,8192]{1,0:T(8,128)(2,1)S(1)} collective-permute-done((bf16[32,8192]{1,0:T(8,128)(2,1)S(1)}, bf16[32,8192]{1,0:T(8,128)(2,1)S(1)}, u32[]{:S(2)}, u32[]{:S(2)}) %collective-permute-start.9) | collective-permute-done | bytes 524320 | tf_op jit(solution)/shard_map/ppermute | solution.py:664
  22.1 1.1 pad_maximum_fusion
  23.2 1.8 collective-permute-start.10
  25.0 19.5 %collective-permute-done.16.refs_1_ = bf16[32,8192]{1,0:T(8,128)(2,1)S(1)} collective-permute-done((bf16[32,8192]{1,0:T(8,128)(2,1)S(1)}, bf16[32,8192]{1,0:T(8,128)(2,1)S(1)}, u32[]{:S(2)}, u32[]{:S(2)}) %collective-permute-start.16) | collective-permute-done | bytes 524320 | tf_op jit(solution)/shard_map/ppermute | solution.py:664
  44.6 1.1 pad_maximum_fusion.1
  45.7 1.7 collective-permute-start.17
  48.1 6.9 %collective-permute-done.23.refs_1_ = bf16[32,8192]{1,0:T(8,128)(2,1)S(1)} collective-permute-done((bf16[32,8192]{1,0:T(8,128)(2,1)S(1)}, bf16[32,8192]{1,0:T(8,128)(2,1)S(1)}, u32[]{:S(2)}, u32[]{:S(2)}) %collective-permute-start.23) | collective-permute-done | bytes 524320 | tf_op jit(solution)/shard_map/ppermute | solution.py:664
  55.0 1.2 pad_maximum_fusion.2
  56.1 1.6 collective-permute-start.24
  58.6 3.2 all-to-all-start
  61.8 1.3 collective-permute-start.3
  63.1 1.3 collective-permute-start.4
  64.5 1.3 collective-permute-start.11
  65.8 1.3 collective-permute-start.18
  67.1 1.0 fusion
  68.1 5.8 %load.3.out_w_ref = bf16[1024,8192]{1,0:T(8,128)(2,1)S(1)} custom-call(bf16[1024,8192]{1,0:T(8,128)(2,1)} %refs_0_.3), custom_call_target="tpu_custom_call" | custom-call | tf_op jit(solution)/shard_map/load/pallas_call | solution.py:288
  73.9 5.8 %copy-done = bf16[1024,8192]{1,0:T(8,128)(2,1)} copy-done((bf16[1024,8192]{1,0:T(8,128)(2,1)}, bf16[1024,8192]{1,0:T(8,128)(2,1)S(1)}, u32[]{:S(2)}) %copy-start) | copy-done | bytes 16777240
  80.1 7.1 %load.2 = (bf16[8192,1024]{1,0:T(8,128)(2,1)S(1)}, bf16[8192,256]{1,0:T(8,128)(2,1)S(1)}) custom-call(bf16[8192,1024]{1,0:T(8,128)(2,1)} %refs_0_.2, bf16[8192,256]{1,0:T(8,128)(2,1)} %refs_1_.1, s32[4]{0:T(128)S(1)} %reduce.refs_2_.labels_ref), custom_call_target="tpu_custom_call" | custom-call | tf_op jit(solution)/shard_map/load/pallas_call | solution.py:288
  87.3 1.6 collective-permute-start.25
  88.8 12.4 %collective-permute-done.4.refs_5_ = bf16[32,8192]{1,0:T(8,128)(2,1)} collective-permute-done((bf16[32,8192]{1,0:T(8,128)(2,1)S(1)}, bf16[32,8192]{1,0:T(8,128)(2,1)}, u32[]{:S(2)}, u32[]{:S(2)}) %collective-permute-start.4) | collective-permute-done | bytes 524320 | tf_op jit(solution)/shard_map/ppermute | solution.py:669
  101.2 7.8 %project.4 = (bf16[128,1024]{1,0:T(8,128)(2,1)S(1)}, bf16[128,256]{1,0:T(8,128)(2,1)S(1)}, bf16[4,128,256]{2,1,0:T(8,128)(2,1)}) custom-call(s32[142]{0:T(256)S(1)} %concatenate.18.info_ref, bf16[32,8192]{1,0:T(8,128)(2,1)} %copy-done.4, bf16[32,8192]{1,0:T(8,128)(2,1)} %copy-done.13, bf16[32,8192]{1,0:T(8,128)(2,1)} %collective-permute-done.1.refs_2_, ...), custom_call_target="tpu_custom_call" | custom-call | flops 2684354560 | bytes 2097152 | tf_op jit(solution)/shard_map/project/pallas_call | solution.py:374
  109.1 9.3 %attend.4 = (bf16[64,8192]{1,0:T(8,128)(2,1)S(1)}, bf16[32,8192]{1,0:T(8,128)(2,1)S(1)}, bf16[32,8192]{1,0:T(8,128)(2,1)S(1)}) custom-call(s32[142]{0:T(256)S(1)} %concatenate.18.info_ref, bf16[128,1024]{1,0:T(8,128)(2,1)S(1)} %get-tuple-element.34.turned_ref, bf16[128,256]{1,0:T(8,128)(2,1)S(1)} %get-tuple-element.35.kept_ref, ...), custom_call_target="tpu_custom_call" | custom-call | flops 4294967296 | bytes 2097152 | tf_op jit(solution)/shard_map/attend/pallas_call | solution.py:522
  118.5 22.0 %collective-permute-start.5 = (bf16[64,8192]{1,0:T(8,128)(2,1)S(1)}, bf16[64,8192]{1,0:T(8,128)(2,1)}, u32[]{:S(2)}, u32[]{:S(2)}) collective-permute-start(bf16[64,8192]{1,0:T(8,128)(2,1)S(1)} %get-tuple-element.37), channel_id=1, source_target_pairs={{0,1},{3,2},{4,5},{7,6},{8,9},{11,10},{12,13},{15,14},{16,17},{19,... | collective-permute-start | bytes 3145736 | tf_op jit(solution)/shard_map/ppermute | solution.py:727
  140.5 5.8 %copy-done.2 = bf16[8192,1024]{1,0:T(8,128)(2,1)S(1)} copy-done((bf16[8192,1024]{1,0:T(8,128)(2,1)S(1)}, bf16[8192,1024]{1,0:T(8,128)(2,1)}, u32[]{:S(2)}) %copy-start.2) | copy-done | bytes 16777240
  146.2 7.5 %project.5 = (bf16[128,1024]{1,0:T(8,128)(2,1)S(1)}, bf16[128,256]{1,0:T(8,128)(2,1)S(1)}, bf16[4,128,256]{2,1,0:T(8,128)(2,1)}) custom-call(s32[142]{0:T(256)S(1)} %concatenate.18.info_ref, bf16[32,8192]{1,0:T(8,128)(2,1)} %copy-done.7, bf16[32,8192]{1,0:T(8,128)(2,1)} %copy-done.10, ...), custom_call_target="tpu_custom_call", output_to_operand_aliasing={{2}: (9, {})} | custom-call | flops 2684354560 | bytes 2097152 | tf_op jit(solution)/shard_map/project/pallas_call | solution.py:374
  153.8 7.6 %project.6 = (bf16[128,1024]{1,0:T(8,128)(2,1)S(1)}, bf16[128,256]{1,0:T(8,128)(2,1)S(1)}, bf16[4,128,256]{2,1,0:T(8,128)(2,1)}) custom-call(s32[142]{0:T(256)S(1)} %concatenate.18.info_ref, bf16[32,8192]{1,0:T(8,128)(2,1)} %copy-done.6, bf16[32,8192]{1,0:T(8,128)(2,1)} %copy-done.11, ...), custom_call_target="tpu_custom_call", output_to_operand_aliasing={{2}: (9, {})} | custom-call | flops 2684354560 | bytes 2097152 | tf_op jit(solution)/shard_map/project/pallas_call | solution.py:374
  161.4 0.8 collective-permute-done.25.refs_3_
  162.2 1.0 copy-done.12
  163.2 7.5 %project.7 = (bf16[128,1024]{1,0:T(8,128)(2,1)S(1)}, bf16[128,256]{1,0:T(8,128)(2,1)S(1)}, bf16[4,128,256]{2,1,0:T(8,128)(2,1)}) custom-call(s32[142]{0:T(256)S(1)} %concatenate.18.info_ref, bf16[32,8192]{1,0:T(8,128)(2,1)} %copy-done.5, bf16[32,8192]{1,0:T(8,128)(2,1)} %copy-done.9, ...), custom_call_target="tpu_custom_call", output_to_operand_aliasing={{2}: (9, {})} | custom-call | flops 2684354560 | bytes 2097152 | tf_op jit(solution)/shard_map/project/pallas_call | solution.py:374
  170.7 6.3 %attend.7 = (bf16[32,8192]{1,0:T(8,128)(2,1)S(1)}, bf16[32,8192]{1,0:T(8,128)(2,1)S(1)}, bf16[32,8192]{1,0:T(8,128)(2,1)S(1)}, bf16[32,8192]{1,0:T(8,128)(2,1)S(1)}) custom-call(s32[142]{0:T(256)S(1)} %concatenate.18.info_ref, bf16[128,1024]{1,0:T(8,128)(2,1)S(1)} %get-tuple-element.55.turned_ref, bf16[128,256]{1,0:T(8,128)(2,1)S(1)} %get-tuple-element.56.kept_ref, ...), custom_call_target="tpu_custom_call" | custom-call | flops 4294967296 | bytes 2097152 | tf_op jit(solution)/shard_map/attend/pallas_call | solution.py:522
  177.0 1.6 collective-permute-start.29
  178.6 1.3 collective-permute-start.27
  180.0 1.3 collective-permute-start.26
  181.3 9.3 %attend.6 = (bf16[64,8192]{1,0:T(8,128)(2,1)S(1)}, bf16[32,8192]{1,0:T(8,128)(2,1)S(1)}, bf16[32,8192]{1,0:T(8,128)(2,1)S(1)}) custom-call(s32[142]{0:T(256)S(1)} %concatenate.18.info_ref, bf16[128,1024]{1,0:T(8,128)(2,1)S(1)} %get-tuple-element.48.turned_ref, bf16[128,256]{1,0:T(8,128)(2,1)S(1)} %get-tuple-element.49.kept_ref, ...), custom_call_target="tpu_custom_call" | custom-call | flops 4294967296 | bytes 2097152 | tf_op jit(solution)/shard_map/attend/pallas_call | solution.py:522
  190.6 1.4 collective-permute-start.19
  192.0 7.1 %attend.5 = (bf16[64,8192]{1,0:T(8,128)(2,1)S(1)}, bf16[32,8192]{1,0:T(8,128)(2,1)S(1)}, bf16[32,8192]{1,0:T(8,128)(2,1)S(1)}) custom-call(s32[142]{0:T(256)S(1)} %concatenate.18.info_ref, bf16[128,1024]{1,0:T(8,128)(2,1)S(1)} %get-tuple-element.41.turned_ref, bf16[128,256]{1,0:T(8,128)(2,1)S(1)} %get-tuple-element.42.kept_ref, ...), custom_call_target="tpu_custom_call" | custom-call | flops 4294967296 | bytes 2097152 | tf_op jit(solution)/shard_map/attend/pallas_call | solution.py:522
  199.1 1.6 collective-permute-start.12
  200.7 1.5 add_convert_fusion.2
  202.2 0.7 collective-permute-start.6
  203.1 0.7 collective-permute-start.30
  203.9 0.7 collective-permute-start.28
  204.8 27.6 %collective-permute-done.19 = bf16[64,8192]{1,0:T(8,128)(2,1)S(1)} collective-permute-done((bf16[64,8192]{1,0:T(8,128)(2,1)S(1)}, bf16[64,8192]{1,0:T(8,128)(2,1)S(1)}, u32[]{:S(2)}, u32[]{:S(2)}) %collective-permute-start.19) | collective-permute-done | bytes 1048608 | tf_op jit(solution)/shard_map/ppermute | solution.py:727
  232.4 1.3 collective-permute-start.31
  233.9 0.7 collective-permute-start.20
  234.8 20.1 %collective-permute-done.12 = bf16[64,8192]{1,0:T(8,128)(2,1)S(1)} collective-permute-done((bf16[64,8192]{1,0:T(8,128)(2,1)S(1)}, bf16[64,8192]{1,0:T(8,128)(2,1)S(1)}, u32[]{:S(2)}, u32[]{:S(2)}) %collective-permute-start.12) | collective-permute-done | bytes 1048608 | tf_op jit(solution)/shard_map/ppermute | solution.py:727
  254.9 2.5 collective-permute-start.7
  257.6 12.5 %collective-permute-done.7 = bf16[32,8192]{1,0:T(8,128)(2,1)S(1)} collective-permute-done((bf16[32,8192]{1,0:T(8,128)(2,1)S(1)}, bf16[32,8192]{1,0:T(8,128)(2,1)S(1)}, u32[]{:S(2)}, u32[]{:S(2)}) %collective-permute-start.7) | collective-permute-done | bytes 524320 | tf_op jit(solution)/shard_map/ppermute | solution.py:729
  270.1 0.7 collective-permute-start.13
  271.3 24.9 %collective-permute-start.21 = (bf16[32,8192]{1,0:T(8,128)(2,1)S(1)}, bf16[32,8192]{1,0:T(8,128)(2,1)S(1)}, u32[]{:S(2)}, u32[]{:S(2)}) collective-permute-start(bf16[32,8192]{1,0:T(8,128)(2,1)S(1)} %add_convert_fusion.7), channel_id=1, source_target_pairs={{0,1},{1,0},{2,3},{3,2},{4,5},{5,4},{6,7},{7,6},{8,9},{9,8},{10,11... | collective-permute-start | bytes 1572872 | tf_op jit(solution)/shard_map/ppermute | solution.py:729
  296.3 11.9 %collective-permute-done.21 = bf16[32,8192]{1,0:T(8,128)(2,1)S(1)} collective-permute-done((bf16[32,8192]{1,0:T(8,128)(2,1)S(1)}, bf16[32,8192]{1,0:T(8,128)(2,1)S(1)}, u32[]{:S(2)}, u32[]{:S(2)}) %collective-permute-start.21) | collective-permute-done | bytes 524320 | tf_op jit(solution)/shard_map/ppermute | solution.py:729
  308.3 2.3 collective-permute-start.14
  310.8 12.1 %collective-permute-done.14 = bf16[32,8192]{1,0:T(8,128)(2,1)S(1)} collective-permute-done((bf16[32,8192]{1,0:T(8,128)(2,1)S(1)}, bf16[32,8192]{1,0:T(8,128)(2,1)S(1)}, u32[]{:S(2)}, u32[]{:S(2)}) %collective-permute-start.14) | collective-permute-done | bytes 524320 | tf_op jit(solution)/shard_map/ppermute | solution.py:729
  323.2 1.6 collective-permute-done.22.refs_2_
  324.8 12.7 %collective-permute-done.15.refs_1_ = bf16[32,8192]{1,0:T(8,128)(2,1)S(1)} collective-permute-done((bf16[32,8192]{1,0:T(8,128)(2,1)S(1)}, bf16[32,8192]{1,0:T(8,128)(2,1)S(1)}, u32[]{:S(2)}, u32[]{:S(2)}) %collective-permute-start.15) | collective-permute-done | bytes 524320 | tf_op jit(solution)/shard_map/ppermute | solution.py:732
  337.5 1.9 finish.1
  (84 shorter events, 4.2 us)
Async XLA Ops:
  2.2 1.6 copy-start.3
  3.8 0.7 copy-start.8
  6.2 17.0 %copy-start.7 = (bf16[32,8192]{1,0:T(8,128)(2,1)}, bf16[32,8192]{1,0:T(8,128)(2,1)S(1)}, u32[]{:S(2)}) copy-start(bf16[32,8192]{1,0:T(8,128)(2,1)S(1)} %get-tuple-element.39.refs_0_) | copy-start | bytes 1572868
  6.2 38.4 %copy-start.6 = (bf16[32,8192]{1,0:T(8,128)(2,1)}, bf16[32,8192]{1,0:T(8,128)(2,1)S(1)}, u32[]{:S(2)}) copy-start(bf16[32,8192]{1,0:T(8,128)(2,1)S(1)} %get-tuple-element.46.refs_0_) | copy-start | bytes 1572868
  6.2 48.8 %copy-start.5 = (bf16[32,8192]{1,0:T(8,128)(2,1)}, bf16[32,8192]{1,0:T(8,128)(2,1)S(1)}, u32[]{:S(2)}) copy-start(bf16[32,8192]{1,0:T(8,128)(2,1)S(1)} %get-tuple-element.53.refs_0_) | copy-start | bytes 1572868
  6.2 15.9 %collective-permute-start.9 = (bf16[32,8192]{1,0:T(8,128)(2,1)S(1)}, bf16[32,8192]{1,0:T(8,128)(2,1)S(1)}, u32[]{:S(2)}, u32[]{:S(2)}) collective-permute-start(bf16[32,8192]{1,0:T(8,128)(2,1)S(1)} %get-tuple-element.39.refs_0_), channel_id=1, source_target_pairs={{0,1},{1,0},{2,3},{3,2},{4,5},{5,4},{6,7},{7,6},{8,9},{9,8},{10,11... | collective-permute-start | bytes 1572872 | tf_op jit(solution)/shard_map/ppermute | solution.py:664
  10.3 35.5 %copy-start.4 = (bf16[32,8192]{1,0:T(8,128)(2,1)}, bf16[32,8192]{1,0:T(8,128)(2,1)S(1)}, u32[]{:S(2)}) copy-start(bf16[32,8192]{1,0:T(8,128)(2,1)S(1)} %norm_some.2.refs_0_) | copy-start | bytes 1572868
  10.3 37.1 %collective-permute-start = (bf16[32,8192]{1,0:T(8,128)(2,1)S(1)}, bf16[32,8192]{1,0:T(8,128)(2,1)S(1)}, u32[]{:S(2)}, u32[]{:S(2)}) collective-permute-start(bf16[32,8192]{1,0:T(8,128)(2,1)S(1)} %norm_some.2.refs_0_), channel_id=1, source_target_pairs={{0,1},{1,0},{2,3},{3,2},{4,5},{5,4},{6,7},{7,6},{8,9},{9,8},{10,11... | collective-permute-start | bytes 1572872 | tf_op jit(solution)/shard_map/ppermute | solution.py:664
  10.3 51.4 %collective-permute-start.1 = (bf16[32,8192]{1,0:T(8,128)(2,1)S(1)}, bf16[32,8192]{1,0:T(8,128)(2,1)}, u32[]{:S(2)}, u32[]{:S(2)}) collective-permute-start(bf16[32,8192]{1,0:T(8,128)(2,1)S(1)} %norm_some.2.refs_0_), channel_id=1, source_target_pairs={{1,2},{2,1},{5,6},{6,5},{9,10},{10,9},{13,14},{14,13},{17,18},{18,... | collective-permute-start | bytes 1572872 | tf_op jit(solution)/shard_map/ppermute | solution.py:666
  11.8 32.8 %collective-permute-start.16 = (bf16[32,8192]{1,0:T(8,128)(2,1)S(1)}, bf16[32,8192]{1,0:T(8,128)(2,1)S(1)}, u32[]{:S(2)}, u32[]{:S(2)}) collective-permute-start(bf16[32,8192]{1,0:T(8,128)(2,1)S(1)} %get-tuple-element.46.refs_0_), channel_id=1, source_target_pairs={{0,1},{1,0},{2,3},{3,2},{4,5},{5,4},{6,7},{7,6},{8,9},{9,8},{10,11... | collective-permute-start | bytes 1572872 | tf_op jit(solution)/shard_map/ppermute | solution.py:664
  15.9 39.1 %collective-permute-start.23 = (bf16[32,8192]{1,0:T(8,128)(2,1)S(1)}, bf16[32,8192]{1,0:T(8,128)(2,1)S(1)}, u32[]{:S(2)}, u32[]{:S(2)}) collective-permute-start(bf16[32,8192]{1,0:T(8,128)(2,1)S(1)} %get-tuple-element.53.refs_0_), channel_id=1, source_target_pairs={{0,1},{1,0},{2,3},{3,2},{4,5},{5,4},{6,7},{7,6},{8,9},{9,8},{10,11... | collective-permute-start | bytes 1572872 | tf_op jit(solution)/shard_map/ppermute | solution.py:664
  22.1 34.0 %copy-start.10 = (bf16[32,8192]{1,0:T(8,128)(2,1)}, bf16[32,8192]{1,0:T(8,128)(2,1)S(1)}, u32[]{:S(2)}) copy-start(bf16[32,8192]{1,0:T(8,128)(2,1)S(1)} %collective-permute-done.9.refs_1_) | copy-start | bytes 1572868
  23.2 34.5 %copy-start.17 = (s32[4]{0:T(128)S(1)}, s32[4]{0:T(128)}, u32[]{:S(2)}) copy-start(s32[4]{0:T(128)} %param.19) | copy-start | bytes 52
  23.2 41.2 %copy-start.16 = (s32[4]{0:T(128)S(1)}, s32[4]{0:T(128)}, u32[]{:S(2)}) copy-start(s32[4]{0:T(128)} %param.17) | copy-start | bytes 52
  23.2 41.3 %collective-permute-start.10 = (bf16[64,8192]{1,0:T(8,128)(2,1)}, bf16[64,8192]{1,0:T(8,128)(2,1)}, u32[]{:S(2)}, u32[]{:S(2)}) collective-permute-start(bf16[64,8192]{1,0:T(8,128)(2,1)} %pad_maximum_fusion), channel_id=1, source_target_pairs={{1,2},{2,1},{5,6},{6,5},{9,10},{10,9},{13,14},{14,13},{17,18},{18,... | collective-permute-start | bytes 3145736 | tf_op jit(solution)/shard_map/ppermute | solution.py:685
  44.6 13.3 %copy-start.11 = (bf16[32,8192]{1,0:T(8,128)(2,1)}, bf16[32,8192]{1,0:T(8,128)(2,1)S(1)}, u32[]{:S(2)}) copy-start(bf16[32,8192]{1,0:T(8,128)(2,1)S(1)} %collective-permute-done.16.refs_1_) | copy-start | bytes 1572868
  45.7 20.1 %collective-permute-start.17 = (bf16[64,8192]{1,0:T(8,128)(2,1)}, bf16[64,8192]{1,0:T(8,128)(2,1)}, u32[]{:S(2)}, u32[]{:S(2)}) collective-permute-start(bf16[64,8192]{1,0:T(8,128)(2,1)} %pad_maximum_fusion.1), channel_id=1, source_target_pairs={{1,2},{2,1},{5,6},{6,5},{9,10},{10,9},{13,14},{14,13},{17,18},{18,... | collective-permute-start | bytes 3145736 | tf_op jit(solution)/shard_map/ppermute | solution.py:685
  47.4 26.5 %copy-start.13 = (bf16[32,8192]{1,0:T(8,128)(2,1)}, bf16[32,8192]{1,0:T(8,128)(2,1)S(1)}, u32[]{:S(2)}) copy-start(bf16[32,8192]{1,0:T(8,128)(2,1)S(1)} %collective-permute-done.refs_1_) | copy-start | bytes 1572868
  47.4 15.7 %collective-permute-start.2 = (bf16[32,8192]{1,0:T(8,128)(2,1)S(1)}, bf16[32,8192]{1,0:T(8,128)(2,1)S(1)}, u32[]{:S(2)}, u32[]{:S(2)}) collective-permute-start(bf16[32,8192]{1,0:T(8,128)(2,1)S(1)} %collective-permute-done.refs_1_), channel_id=1, source_target_pairs={{1,2},{2,1},{5,6},{6,5},{9,10},{10,9},{13,14},{14,13},{17,18},{18,... | collective-permute-start | bytes 1572872 | tf_op jit(solution)/shard_map/ppermute | solution.py:667
  55.0 18.9 %copy-start.9 = (bf16[32,8192]{1,0:T(8,128)(2,1)}, bf16[32,8192]{1,0:T(8,128)(2,1)S(1)}, u32[]{:S(2)}) copy-start(bf16[32,8192]{1,0:T(8,128)(2,1)S(1)} %collective-permute-done.23.refs_1_) | copy-start | bytes 1572868
  56.1 31.1 %collective-permute-start.24 = (bf16[64,8192]{1,0:T(8,128)(2,1)}, bf16[64,8192]{1,0:T(8,128)(2,1)}, u32[]{:S(2)}, u32[]{:S(2)}) collective-permute-start(bf16[64,8192]{1,0:T(8,128)(2,1)} %pad_maximum_fusion.2), channel_id=1, source_target_pairs={{1,2},{2,1},{5,6},{6,5},{9,10},{10,9},{13,14},{14,13},{17,18},{18,... | collective-permute-start | bytes 3145736 | tf_op jit(solution)/shard_map/ppermute | solution.py:685
  58.6 21.4 %all-to-all-start = ((s32[4,1,1]{2,1,0:T(1,128)}), s32[4,1,1]{2,1,0:T(1,128)S(1)}, u32[]{:S(2)}, u32[]{:S(2)}) async-start(s32[4,1,1]{2,1,0:T(1,128)} %copy.17), calls=%async_computation | async-start | bytes 4096 | tf_op jit(solution)/shard_map/all_to_all | solution.py:656
  61.8 27.0 %collective-permute-start.3 = (bf16[32,8192]{1,0:T(8,128)(2,1)}, bf16[32,8192]{1,0:T(8,128)(2,1)S(1)}, u32[]{:S(2)}, u32[]{:S(2)}) collective-permute-start(bf16[32,8192]{1,0:T(8,128)(2,1)} %collective-permute-done.1.refs_2_), channel_id=1, source_target_pairs={{1,0},{2,3},{5,4},{6,7},{9,8},{10,11},{13,12},{14,15},{17,16},{18,... | collective-permute-start | bytes 1572872 | tf_op jit(solution)/shard_map/ppermute | solution.py:668
  63.1 10.8 %copy-start.14 = (bf16[32,8192]{1,0:T(8,128)(2,1)}, bf16[32,8192]{1,0:T(8,128)(2,1)S(1)}, u32[]{:S(2)}) copy-start(bf16[32,8192]{1,0:T(8,128)(2,1)S(1)} %collective-permute-done.2.refs_3_) | copy-start | bytes 1572868
  63.1 38.1 %collective-permute-start.4 = (bf16[32,8192]{1,0:T(8,128)(2,1)S(1)}, bf16[32,8192]{1,0:T(8,128)(2,1)}, u32[]{:S(2)}, u32[]{:S(2)}) collective-permute-start(bf16[32,8192]{1,0:T(8,128)(2,1)S(1)} %collective-permute-done.2.refs_3_), channel_id=1, source_target_pairs={{1,0},{2,3},{5,4},{6,7},{9,8},{10,11},{13,12},{14,15},{17,16},{18,... | collective-permute-start | bytes 1572872 | tf_op jit(solution)/shard_map/ppermute | solution.py:669
  64.5 76.0 %collective-permute-start.11 = (bf16[64,8192]{1,0:T(8,128)(2,1)}, bf16[64,8192]{1,0:T(8,128)(2,1)}, u32[]{:S(2)}, u32[]{:S(2)}) collective-permute-start(bf16[64,8192]{1,0:T(8,128)(2,1)} %collective-permute-done.10.refs_2_), channel_id=1, source_target_pairs={{1,0},{2,3},{5,4},{6,7},{9,8},{10,11},{13,12},{14,15},{17,16},{18,... | collective-permute-start | bytes 3145736 | tf_op jit(solution)/shard_map/ppermute | solution.py:686
  65.8 88.0 %collective-permute-start.18 = (bf16[64,8192]{1,0:T(8,128)(2,1)}, bf16[64,8192]{1,0:T(8,128)(2,1)}, u32[]{:S(2)}, u32[]{:S(2)}) collective-permute-start(bf16[64,8192]{1,0:T(8,128)(2,1)} %collective-permute-done.17.refs_2_), channel_id=1, source_target_pairs={{1,0},{2,3},{5,4},{6,7},{9,8},{10,11},{13,12},{14,15},{17,16},{18,... | collective-permute-start | bytes 3145736 | tf_op jit(solution)/shard_map/ppermute | solution.py:686
  73.9 5.8 %copy-start = (bf16[1024,8192]{1,0:T(8,128)(2,1)}, bf16[1024,8192]{1,0:T(8,128)(2,1)S(1)}, u32[]{:S(2)}) copy-start(bf16[1024,8192]{1,0:T(8,128)(2,1)S(1)} %load.3.out_w_ref) | copy-start | bytes 50331652
  80.1 29.0 %slice-start = ((s8[16777216]{0:T(1024)(128)(4,1)}), s8[4194304]{0:T(1024)(128)(4,1)S(1)}, s32[]{:S(2)}) async-start(s8[16777216]{0:T(1024)(128)(4,1)} %bitcast.4), calls=%async_computation.1 | async-start | bytes 8388608
  80.1 29.0 %slice-start.1 = ((s8[16777216]{0:T(1024)(128)(4,1)}), s8[4194304]{0:T(1024)(128)(4,1)S(1)}, s32[]{:S(2)}) async-start(s8[16777216]{0:T(1024)(128)(4,1)} %bitcast.4), calls=%async_computation.2 | async-start | bytes 8388608
  87.2 21.9 %copy-start.1 = (bf16[8192,1024]{1,0:T(8,128)(2,1)}, bf16[8192,1024]{1,0:T(8,128)(2,1)S(1)}, u32[]{:S(2)}) copy-start(bf16[8192,1024]{1,0:T(8,128)(2,1)S(1)} %get-tuple-element.32.refs_6_.refs_4_) | copy-start | bytes 50331652
  87.3 74.9 %collective-permute-start.25 = (bf16[64,8192]{1,0:T(8,128)(2,1)}, bf16[64,8192]{1,0:T(8,128)(2,1)S(1)}, u32[]{:S(2)}, u32[]{:S(2)}) collective-permute-start(bf16[64,8192]{1,0:T(8,128)(2,1)} %collective-permute-done.24.refs_2_), channel_id=1, source_target_pairs={{1,0},{2,3},{5,4},{6,7},{9,8},{10,11},{13,12},{14,15},{17,16},{18,... | collective-permute-start | bytes 3145736 | tf_op jit(solution)/shard_map/ppermute | solution.py:686
  88.8 12.4 %copy-start.15 = (bf16[32,8192]{1,0:T(8,128)(2,1)}, bf16[32,8192]{1,0:T(8,128)(2,1)S(1)}, u32[]{:S(2)}) copy-start(bf16[32,8192]{1,0:T(8,128)(2,1)S(1)} %collective-permute-done.3.refs_4_) | copy-start | bytes 1572868
  101.2 7.9 %slice-start.2 = ((s8[16777216]{0:T(1024)(128)(4,1)}), s8[4194304]{0:T(1024)(128)(4,1)S(1)}, s32[]{:S(2)}) async-start(s8[16777216]{0:T(1024)(128)(4,1)} %bitcast.4), calls=%async_computation.3 | async-start | bytes 8388608
  101.2 7.9 %slice-start.3 = ((s8[16777216]{0:T(1024)(128)(4,1)}), s8[4194304]{0:T(1024)(128)(4,1)S(1)}, s32[]{:S(2)}) async-start(s8[16777216]{0:T(1024)(128)(4,1)} %bitcast.4), calls=%async_computation.4 | async-start | bytes 8388608
  118.5 80.6 %collective-permute-start.5 = (bf16[64,8192]{1,0:T(8,128)(2,1)S(1)}, bf16[64,8192]{1,0:T(8,128)(2,1)}, u32[]{:S(2)}, u32[]{:S(2)}) collective-permute-start(bf16[64,8192]{1,0:T(8,128)(2,1)S(1)} %get-tuple-element.37), channel_id=1, source_target_pairs={{0,1},{3,2},{4,5},{7,6},{8,9},{11,10},{12,13},{15,14},{16,17},{19,... | collective-permute-start | bytes 3145736 | tf_op jit(solution)/shard_map/ppermute | solution.py:727
  140.5 5.8 %copy-start.2 = (bf16[8192,1024]{1,0:T(8,128)(2,1)S(1)}, bf16[8192,1024]{1,0:T(8,128)(2,1)}, u32[]{:S(2)}) copy-start(bf16[8192,1024]{1,0:T(8,128)(2,1)} %copy-done.1) | copy-start | bytes 50331652
  162.2 1.0 copy-start.12
  177.0 25.2 %collective-permute-start.29 = (bf16[32,8192]{1,0:T(8,128)(2,1)S(1)}, bf16[32,8192]{1,0:T(8,128)(2,1)S(1)}, u32[]{:S(2)}, u32[]{:S(2)}) collective-permute-start(bf16[32,8192]{1,0:T(8,128)(2,1)S(1)} %get-tuple-element.59), channel_id=1, source_target_pairs={{0,1},{3,2},{4,5},{7,6},{8,9},{11,10},{12,13},{15,14},{16,17},{19,... | collective-permute-start | bytes 1572872 | tf_op jit(solution)/shard_map/ppermute | solution.py:718
  178.6 24.4 %collective-permute-start.27 = (bf16[32,8192]{1,0:T(8,128)(2,1)S(1)}, bf16[32,8192]{1,0:T(8,128)(2,1)S(1)}, u32[]{:S(2)}, u32[]{:S(2)}) collective-permute-start(bf16[32,8192]{1,0:T(8,128)(2,1)S(1)} %get-tuple-element.60), channel_id=1, source_target_pairs={{0,1},{3,2},{4,5},{7,6},{8,9},{11,10},{12,13},{15,14},{16,17},{19,... | collective-permute-start | bytes 1572872 | tf_op jit(solution)/shard_map/ppermute | solution.py:719
  180.0 143.1 %collective-permute-start.26 = (bf16[32,8192]{1,0:T(8,128)(2,1)S(1)}, bf16[32,8192]{1,0:T(8,128)(2,1)S(1)}, u32[]{:S(2)}, u32[]{:S(2)}) collective-permute-start(bf16[32,8192]{1,0:T(8,128)(2,1)S(1)} %get-tuple-element.58), channel_id=1, source_target_pairs={{0,1},{3,2},{4,5},{7,6},{8,9},{11,10},{12,13},{15,14},{16,17},{19,... | collective-permute-start | bytes 1572872 | tf_op jit(solution)/shard_map/ppermute | solution.py:720
  190.6 41.8 %collective-permute-start.19 = (bf16[64,8192]{1,0:T(8,128)(2,1)S(1)}, bf16[64,8192]{1,0:T(8,128)(2,1)S(1)}, u32[]{:S(2)}, u32[]{:S(2)}) collective-permute-start(bf16[64,8192]{1,0:T(8,128)(2,1)S(1)} %get-tuple-element.51), channel_id=1, source_target_pairs={{0,1},{3,2},{4,5},{7,6},{8,9},{11,10},{12,13},{15,14},{16,17},{19,... | collective-permute-start | bytes 3145736 | tf_op jit(solution)/shard_map/ppermute | solution.py:727
  199.1 55.7 %collective-permute-start.12 = (bf16[64,8192]{1,0:T(8,128)(2,1)S(1)}, bf16[64,8192]{1,0:T(8,128)(2,1)S(1)}, u32[]{:S(2)}, u32[]{:S(2)}) collective-permute-start(bf16[64,8192]{1,0:T(8,128)(2,1)S(1)} %get-tuple-element.44), channel_id=1, source_target_pairs={{0,1},{3,2},{4,5},{7,6},{8,9},{11,10},{12,13},{15,14},{16,17},{19,... | collective-permute-start | bytes 3145736 | tf_op jit(solution)/shard_map/ppermute | solution.py:727
  202.2 31.7 %collective-permute-start.6 = (bf16[64,8192]{1,0:T(8,128)(2,1)S(1)}, bf16[64,8192]{1,0:T(8,128)(2,1)S(1)}, u32[]{:S(2)}, u32[]{:S(2)}) collective-permute-start(bf16[64,8192]{1,0:T(8,128)(2,1)S(1)} %add_convert_fusion.2), channel_id=1, source_target_pairs={{1,2},{2,1},{5,6},{6,5},{9,10},{10,9},{13,14},{14,13},{17,18},{18,... | collective-permute-start | bytes 3145736 | tf_op jit(solution)/shard_map/ppermute | solution.py:728
  203.1 0.8 collective-permute-start.30
  203.9 119.3 %collective-permute-start.28 = (bf16[32,8192]{1,0:T(8,128)(2,1)S(1)}, bf16[32,8192]{1,0:T(8,128)(2,1)S(1)}, u32[]{:S(2)}, u32[]{:S(2)}) collective-permute-start(bf16[32,8192]{1,0:T(8,128)(2,1)S(1)} %add_convert_fusion.5), channel_id=1, source_target_pairs={{1,2},{2,1},{5,6},{6,5},{9,10},{10,9},{13,14},{14,13},{17,18},{18,... | collective-permute-start | bytes 1572872 | tf_op jit(solution)/shard_map/ppermute | solution.py:722
  232.4 90.8 %collective-permute-start.31 = (bf16[32,8192]{1,0:T(8,128)(2,1)S(1)}, bf16[32,8192]{1,0:T(8,128)(2,1)S(1)}, u32[]{:S(2)}, u32[]{:S(2)}) collective-permute-start(bf16[32,8192]{1,0:T(8,128)(2,1)S(1)} %add_convert_fusion.3), channel_id=1, source_target_pairs={{1,0},{2,3},{5,4},{6,7},{9,8},{10,11},{13,12},{14,15},{17,16},{18,... | collective-permute-start | bytes 1572872 | tf_op jit(solution)/shard_map/ppermute | solution.py:723
  233.9 37.1 %collective-permute-start.20 = (bf16[64,8192]{1,0:T(8,128)(2,1)S(1)}, bf16[64,8192]{1,0:T(8,128)(2,1)S(1)}, u32[]{:S(2)}, u32[]{:S(2)}) collective-permute-start(bf16[64,8192]{1,0:T(8,128)(2,1)S(1)} %add_convert_fusion), channel_id=1, source_target_pairs={{1,2},{2,1},{5,6},{6,5},{9,10},{10,9},{13,14},{14,13},{17,18},{18,... | collective-permute-start | bytes 3145736 | tf_op jit(solution)/shard_map/ppermute | solution.py:728
  254.9 15.3 %collective-permute-start.7 = (bf16[32,8192]{1,0:T(8,128)(2,1)S(1)}, bf16[32,8192]{1,0:T(8,128)(2,1)S(1)}, u32[]{:S(2)}, u32[]{:S(2)}) collective-permute-start(bf16[32,8192]{1,0:T(8,128)(2,1)S(1)} %add_convert_fusion.11), channel_id=1, source_target_pairs={{0,1},{1,0},{2,3},{3,2},{4,5},{5,4},{6,7},{7,6},{8,9},{9,8},{10,11... | collective-permute-start | bytes 1572872 | tf_op jit(solution)/shard_map/ppermute | solution.py:729
  270.1 1.2 collective-permute-start.13
  271.1 52.2 %collective-permute-start.8 = (bf16[32,8192]{1,0:T(8,128)(2,1)S(1)}, bf16[32,8192]{1,0:T(8,128)(2,1)S(1)}, u32[]{:S(2)}, u32[]{:S(2)}) collective-permute-start(bf16[32,8192]{1,0:T(8,128)(2,1)S(1)} %add_convert_fusion.10), channel_id=1, source_target_pairs={{0,12},{4,8},{8,4},{12,0},{1,13},{5,9},{9,5},{13,1},{2,14},{6,10},... | collective-permute-start | bytes 1572872 | tf_op jit(solution)/shard_map/ppermute | solution.py:732
  271.3 37.0 %collective-permute-start.21 = (bf16[32,8192]{1,0:T(8,128)(2,1)S(1)}, bf16[32,8192]{1,0:T(8,128)(2,1)S(1)}, u32[]{:S(2)}, u32[]{:S(2)}) collective-permute-start(bf16[32,8192]{1,0:T(8,128)(2,1)S(1)} %add_convert_fusion.7), channel_id=1, source_target_pairs={{0,1},{1,0},{2,3},{3,2},{4,5},{5,4},{6,7},{7,6},{8,9},{9,8},{10,11... | collective-permute-start | bytes 1572872 | tf_op jit(solution)/shard_map/ppermute | solution.py:729
  308.3 14.6 %collective-permute-start.14 = (bf16[32,8192]{1,0:T(8,128)(2,1)S(1)}, bf16[32,8192]{1,0:T(8,128)(2,1)S(1)}, u32[]{:S(2)}, u32[]{:S(2)}) collective-permute-start(bf16[32,8192]{1,0:T(8,128)(2,1)S(1)} %add_convert_fusion.9), channel_id=1, source_target_pairs={{0,1},{1,0},{2,3},{3,2},{4,5},{5,4},{6,7},{7,6},{8,9},{9,8},{10,11... | collective-permute-start | bytes 1572872 | tf_op jit(solution)/shard_map/ppermute | solution.py:729
  322.9 1.9 collective-permute-start.22
  323.1 14.4 %collective-permute-start.15 = (bf16[32,8192]{1,0:T(8,128)(2,1)S(1)}, bf16[32,8192]{1,0:T(8,128)(2,1)S(1)}, u32[]{:S(2)}, u32[]{:S(2)}) collective-permute-start(bf16[32,8192]{1,0:T(8,128)(2,1)S(1)} %add_convert_fusion.8), channel_id=1, source_target_pairs={{0,8},{4,12},{8,0},{12,4},{1,9},{5,13},{9,1},{13,5},{2,10},{6,14},... | collective-permute-start | bytes 1572872 | tf_op jit(solution)/shard_map/ppermute | solution.py:732

commit v2 on v1

--- a/solution.py
+++ b/solution.py
@@ -219,6 +219,8 @@
 
 
 LINE = 4
+CHUNK = 128
+GROUP = 4
 
 
 def pick_of(info_ref, turn, holding):
@@ -435,28 +437,31 @@
         page_copy(place).start()
 
     def fold(keys, values, mask):
-        scores = jnp.dot(keys, turned_ref[...], preferred_element_type=jnp.float32)
-        if mask is not None:
-            scores = jnp.where(mask, scores, MASKED)
-            top = jnp.max(scores, axis=0, keepdims=True)
-        else:
-            top = jnp.maximum(top_ref[...], jnp.max(scores, axis=0, keepdims=True))
-        exps = jnp.exp2((scores - top) * scale)
-        summed = jnp.sum(exps, axis=0, keepdims=True)
-        taken = lax.dot_general(
-            values, exps.astype(jnp.bfloat16), (((0,), (0,)), ((), ())), preferred_element_type=jnp.float32
-        )
-        if mask is not None:
-            sum_ref[...] = summed
-            acc_ref[...] = taken
-        else:
-            fade = jnp.exp2((top_ref[...] - top) * scale)
-            sum_ref[...] = sum_ref[...] * fade + summed
-            acc_ref[...] = acc_ref[...] * fade + taken
-        top_ref[...] = top
-
-    key_row = lax.broadcasted_iota(jnp.int32, (length, lanes), 0)
-    query_row = lax.rem(lax.broadcasted_iota(jnp.int32, (length, lanes), 1), length)
+        for first in range(0, lanes, chunk):
+            span = slice(first, first + chunk)
+            scores = jnp.dot(keys, turned_ref[:, span], preferred_element_type=jnp.float32)
+            if mask is not None:
+                scores = jnp.where(mask, scores, MASKED)
+                top = jnp.max(scores, axis=0, keepdims=True)
+            else:
+                top = jnp.maximum(top_ref[:, span], jnp.max(scores, axis=0, keepdims=True))
+            exps = jnp.exp2((scores - top) * scale)
+            summed = jnp.sum(exps, axis=0, keepdims=True)
+            taken = lax.dot_general(
+                values, exps.astype(jnp.bfloat16), (((0,), (0,)), ((), ())), preferred_element_type=jnp.float32
+            )
+            if mask is not None:
+                sum_ref[:, span] = summed
+                acc_ref[:, span] = taken
+            else:
+                fade = jnp.exp2((top_ref[:, span] - top) * scale)
+                sum_ref[:, span] = sum_ref[:, span] * fade + summed
+                acc_ref[:, span] = acc_ref[:, span] * fade + taken
+            top_ref[:, span] = top
+
+    chunk = min(lanes, CHUNK)
+    key_row = lax.broadcasted_iota(jnp.int32, (length, chunk), 0)
+    query_row = lax.rem(lax.broadcasted_iota(jnp.int32, (length, chunk), 1), length)
     fold(kept_ref[:, :head_width], kept_ref[:, head_width:], (key_row <= query_row) & (key_row < live))
 
     def fold_span(first, span):
@@ -518,7 +523,7 @@
     inner, width = w_out.shape
     tile = min(width, 1024)
     tiles = width // tile
-    group = min(4, limit)
+    group = min(GROUP, limit)
     return pl.pallas_call(
         functools.partial(
             stretch_kernel, len(sizes), part, pieces, turn, holding, limit, length, group, tile
@@ -726,8 +731,10 @@
             far_part, beside, own = parts
             joined = lax.ppermute(far_part, "tp", inward)
             crossed = lax.ppermute(added(far_part, joined), "tp", middle)
-            swapped = lax.ppermute(added(beside, crossed[share:]), "tp", sides)
-            branch = added(own, crossed[:share], swapped)
+            from_outer = lax.ppermute(beside, "tp", inward)
+            outgoing = added(beside, crossed[share:])
+            from_inner = lax.ppermute(outgoing, "tp", outward)
+            branch = added(own, crossed[:share], from_outer, from_inner)
             pairs = [(g, g ^ turn) for g in range(groups)]
             arrived.append(lax.ppermute(branch, "dp", pairs))
     return (result, placed)

time: 341 us -> 425 us (1.25)
  waiting for transfers between devices: 144 us -> 248 us
  starting transfers between devices: 88.4 us -> 70.2 us
    ppermute x3 -> x6, waiting for transfers between devices: 36.6 us -> 130 us  [the longest x3 130 us: paired(): from_inner = lax.ppermute(outgoing, 'tp', outward)]
    ppermute x3 -> x6, starting transfers between devices: 29.7 us -> 11.1 us  [the longest x3 7.23 us: paired(): from_outer = lax.ppermute(beside, 'tp', inward)]
    ppermute x3, waiting for transfers between devices: 47.7 us -> 58.2 us  [paired(): joined = lax.ppermute(far_part, 'tp', inward)]
  transfers between devices with their start and end apart: 33 -> 36, of which waited for: 12 -> 12; matrix products, arithmetic and copies ran while one was open for 3% -> 2% of each run, Pallas kernels for 22% -> 18%
where the time goes in v2:
time: 425 us; the launch traced here: 424 us
  waiting for transfers between devices  248 us (58%)
  Pallas kernels  79.7 us (19%)
  starting transfers between devices  70.2 us (17%)
  local copies, waits for them, and re-layouts  17.1 us (4%)
  other arithmetic  7.22 us (2%)
    ppermute x3, waiting for transfers between devices, paired(): from_inner = lax.ppermute(outgoing, 'tp', outward)  130 us
    ppermute x3, waiting for transfers between devices, paired(): joined = lax.ppermute(far_part, 'tp', inward)  58.2 us
    ppermute x4, waiting for transfers between devices, paired(): sibling = lax.ppermute(own, 'tp', sides)  32.5 us
    pallas_call x4, Pallas kernels, attend_stretch(): pl.pallas_call(functools.partial(stretch_kernel, len(sizes), part, pieces...  31.7 us
    pallas_call x4, Pallas kernels, project(): pl.pallas_call(functools.partial(project_kernel, len(sources), share, pla...  30.5 us
    ppermute x3, starting transfers between devices, paired(): joined = lax.ppermute(far_part, 'tp', inward)  25.2 us
    unnamed x44, local copies, waits for them, and re-layouts  14.9 us
    ppermute x3, waiting for transfers between devices, paired(): arrived.append(lax.ppermute(branch, 'dp', pairs))  14.2 us
  transfers between devices with their start and end apart: 36, of which 12 were waited for; matrix products, arithmetic and copies ran while one was open for 2% of the time, Pallas kernels for 18%

profile of v2, /device:TPU:0, one launch (start us, length us, event | category | flops | bytes accessed | tf_op | source)
XLA Modules:
  0.0 423.6 jit_solution(6986992242424151285)
XLA Ops:
  0.6 0.8 reshape.41
  1.4 0.8 concatenate.18.info_ref
  2.2 1.6 copy-done.3
  3.8 0.7 copy-done.8
  4.5 1.7 norm_some.3
  6.2 3.1 collective-permute-start.10
  9.3 0.9 norm_some.2.refs_0_
  10.3 1.5 collective-permute-start.1
  11.8 4.1 collective-permute-start.18
  16.0 6.1 %collective-permute-done.10.refs_1_ = bf16[32,8192]{1,0:T(8,128)(2,1)S(1)} collective-permute-done((bf16[32,8192]{1,0:T(8,128)(2,1)S(1)}, bf16[32,8192]{1,0:T(8,128)(2,1)S(1)}, u32[]{:S(2)}, u32[]{:S(2)}) %collective-permute-start.10) | collective-permute-done | bytes 524320 | tf_op jit(solution)/shard_map/ppermute | solution.py:669
  22.1 1.1 pad_maximum_fusion
  23.2 1.8 collective-permute-start.11
  25.1 19.5 %collective-permute-done.18.refs_1_ = bf16[32,8192]{1,0:T(8,128)(2,1)S(1)} collective-permute-done((bf16[32,8192]{1,0:T(8,128)(2,1)S(1)}, bf16[32,8192]{1,0:T(8,128)(2,1)S(1)}, u32[]{:S(2)}, u32[]{:S(2)}) %collective-permute-start.18) | collective-permute-done | bytes 524320 | tf_op jit(solution)/shard_map/ppermute | solution.py:669
  44.6 1.1 pad_maximum_fusion.1
  45.7 1.7 collective-permute-start.19
  48.1 6.9 %collective-permute-done.26.refs_1_ = bf16[32,8192]{1,0:T(8,128)(2,1)S(1)} collective-permute-done((bf16[32,8192]{1,0:T(8,128)(2,1)S(1)}, bf16[32,8192]{1,0:T(8,128)(2,1)S(1)}, u32[]{:S(2)}, u32[]{:S(2)}) %collective-permute-start.26) | collective-permute-done | bytes 524320 | tf_op jit(solution)/shard_map/ppermute | solution.py:669
  55.0 1.1 pad_maximum_fusion.2
  56.1 1.6 collective-permute-start.27
  58.5 3.2 all-to-all-start
  61.8 1.3 collective-permute-start.3
  63.1 1.3 collective-permute-start.4
  64.5 1.3 collective-permute-start.12
  65.8 1.3 collective-permute-start.20
  67.1 1.0 fusion
  68.1 5.8 %load.3.out_w_ref = bf16[1024,8192]{1,0:T(8,128)(2,1)S(1)} custom-call(bf16[1024,8192]{1,0:T(8,128)(2,1)} %refs_0_.3), custom_call_target="tpu_custom_call" | custom-call | tf_op jit(solution)/shard_map/load/pallas_call | solution.py:290
  73.9 5.8 %copy-done = bf16[1024,8192]{1,0:T(8,128)(2,1)} copy-done((bf16[1024,8192]{1,0:T(8,128)(2,1)}, bf16[1024,8192]{1,0:T(8,128)(2,1)S(1)}, u32[]{:S(2)}) %copy-start) | copy-done | bytes 16777240
  80.1 7.1 %load.2 = (bf16[8192,1024]{1,0:T(8,128)(2,1)S(1)}, bf16[8192,256]{1,0:T(8,128)(2,1)S(1)}) custom-call(bf16[8192,1024]{1,0:T(8,128)(2,1)} %refs_0_.2, bf16[8192,256]{1,0:T(8,128)(2,1)} %refs_1_.1, s32[4]{0:T(128)S(1)} %reduce.refs_2_.labels_ref), custom_call_target="tpu_custom_call" | custom-call | tf_op jit(solution)/shard_map/load/pallas_call | solution.py:290
  87.2 1.6 collective-permute-start.28
  88.8 12.4 %collective-permute-done.4.refs_5_ = bf16[32,8192]{1,0:T(8,128)(2,1)} collective-permute-done((bf16[32,8192]{1,0:T(8,128)(2,1)S(1)}, bf16[32,8192]{1,0:T(8,128)(2,1)}, u32[]{:S(2)}, u32[]{:S(2)}) %collective-permute-start.4) | collective-permute-done | bytes 524320 | tf_op jit(solution)/shard_map/ppermute | solution.py:674
  101.3 7.8 %project.4 = (bf16[128,1024]{1,0:T(8,128)(2,1)S(1)}, bf16[128,256]{1,0:T(8,128)(2,1)S(1)}, bf16[4,128,256]{2,1,0:T(8,128)(2,1)}) custom-call(s32[142]{0:T(256)S(1)} %concatenate.18.info_ref, bf16[32,8192]{1,0:T(8,128)(2,1)} %copy-done.4, bf16[32,8192]{1,0:T(8,128)(2,1)} %copy-done.13, bf16[32,8192]{1,0:T(8,128)(2,1)} %collective-permute-done.1.refs_2_, ...), custom_call_target="tpu_custom_call" | custom-call | flops 2684354560 | bytes 2097152 | tf_op jit(solution)/shard_map/project/pallas_call | solution.py:376
  109.2 9.1 %attend.4 = (bf16[64,8192]{1,0:T(8,128)(2,1)S(1)}, bf16[32,8192]{1,0:T(8,128)(2,1)S(1)}, bf16[32,8192]{1,0:T(8,128)(2,1)S(1)}) custom-call(s32[142]{0:T(256)S(1)} %concatenate.18.info_ref, bf16[128,1024]{1,0:T(8,128)(2,1)S(1)} %get-tuple-element.34.turned_ref, bf16[128,256]{1,0:T(8,128)(2,1)S(1)} %get-tuple-element.35.kept_ref, ...), custom_call_target="tpu_custom_call" | custom-call | flops 4294967296 | bytes 2097152 | tf_op jit(solution)/shard_map/attend/pallas_call | solution.py:527
  118.3 21.0 %collective-permute-start.5 = (bf16[64,8192]{1,0:T(8,128)(2,1)S(1)}, bf16[64,8192]{1,0:T(8,128)(2,1)S(1)}, u32[]{:S(2)}, u32[]{:S(2)}) collective-permute-start(bf16[64,8192]{1,0:T(8,128)(2,1)S(1)} %get-tuple-element.37), channel_id=1, source_target_pairs={{0,1},{3,2},{4,5},{7,6},{8,9},{11,10},{12,13},{15,14},{16,17},{19,... | collective-permute-start | bytes 3145736 | tf_op jit(solution)/shard_map/ppermute | solution.py:732
  139.3 1.5 collective-permute-start.7
  140.8 5.8 %copy-done.2 = bf16[8192,1024]{1,0:T(8,128)(2,1)S(1)} copy-done((bf16[8192,1024]{1,0:T(8,128)(2,1)S(1)}, bf16[8192,1024]{1,0:T(8,128)(2,1)}, u32[]{:S(2)}) %copy-start.2) | copy-done | bytes 16777240
  146.6 7.6 %project.5 = (bf16[128,1024]{1,0:T(8,128)(2,1)S(1)}, bf16[128,256]{1,0:T(8,128)(2,1)S(1)}, bf16[4,128,256]{2,1,0:T(8,128)(2,1)}) custom-call(s32[142]{0:T(256)S(1)} %concatenate.18.info_ref, bf16[32,8192]{1,0:T(8,128)(2,1)} %copy-done.7, bf16[32,8192]{1,0:T(8,128)(2,1)} %copy-done.10, ...), custom_call_target="tpu_custom_call", output_to_operand_aliasing={{2}: (9, {})} | custom-call | flops 2684354560 | bytes 2097152 | tf_op jit(solution)/shard_map/project/pallas_call | solution.py:376
  154.2 7.6 %project.6 = (bf16[128,1024]{1,0:T(8,128)(2,1)S(1)}, bf16[128,256]{1,0:T(8,128)(2,1)S(1)}, bf16[4,128,256]{2,1,0:T(8,128)(2,1)}) custom-call(s32[142]{0:T(256)S(1)} %concatenate.18.info_ref, bf16[32,8192]{1,0:T(8,128)(2,1)} %copy-done.6, bf16[32,8192]{1,0:T(8,128)(2,1)} %copy-done.11, ...), custom_call_target="tpu_custom_call", output_to_operand_aliasing={{2}: (9, {})} | custom-call | flops 2684354560 | bytes 2097152 | tf_op jit(solution)/shard_map/project/pallas_call | solution.py:376
  162.2 1.0 copy-done.12
  163.2 7.5 %project.7 = (bf16[128,1024]{1,0:T(8,128)(2,1)S(1)}, bf16[128,256]{1,0:T(8,128)(2,1)S(1)}, bf16[4,128,256]{2,1,0:T(8,128)(2,1)}) custom-call(s32[142]{0:T(256)S(1)} %concatenate.18.info_ref, bf16[32,8192]{1,0:T(8,128)(2,1)} %copy-done.5, bf16[32,8192]{1,0:T(8,128)(2,1)} %copy-done.9, ...), custom_call_target="tpu_custom_call", output_to_operand_aliasing={{2}: (9, {})} | custom-call | flops 2684354560 | bytes 2097152 | tf_op jit(solution)/shard_map/project/pallas_call | solution.py:376
  170.7 6.2 %attend.7 = (bf16[32,8192]{1,0:T(8,128)(2,1)S(1)}, bf16[32,8192]{1,0:T(8,128)(2,1)S(1)}, bf16[32,8192]{1,0:T(8,128)(2,1)S(1)}, bf16[32,8192]{1,0:T(8,128)(2,1)S(1)}) custom-call(s32[142]{0:T(256)S(1)} %concatenate.18.info_ref, bf16[128,1024]{1,0:T(8,128)(2,1)S(1)} %get-tuple-element.55.turned_ref, bf16[128,256]{1,0:T(8,128)(2,1)S(1)} %get-tuple-element.56.kept_ref, ...), custom_call_target="tpu_custom_call" | custom-call | flops 4294967296 | bytes 2097152 | tf_op jit(solution)/shard_map/attend/pallas_call | solution.py:527
  177.0 1.6 collective-permute-start.32
  178.6 1.3 collective-permute-start.30
  179.9 1.3 collective-permute-start.29
  181.3 9.1 %attend.6 = (bf16[64,8192]{1,0:T(8,128)(2,1)S(1)}, bf16[32,8192]{1,0:T(8,128)(2,1)S(1)}, bf16[32,8192]{1,0:T(8,128)(2,1)S(1)}) custom-call(s32[142]{0:T(256)S(1)} %concatenate.18.info_ref, bf16[128,1024]{1,0:T(8,128)(2,1)S(1)} %get-tuple-element.48.turned_ref, bf16[128,256]{1,0:T(8,128)(2,1)S(1)} %get-tuple-element.49.kept_ref, ...), custom_call_target="tpu_custom_call" | custom-call | flops 4294967296 | bytes 2097152 | tf_op jit(solution)/shard_map/attend/pallas_call | solution.py:527
  190.4 1.4 collective-permute-start.21
  192.0 7.3 %attend.5 = (bf16[64,8192]{1,0:T(8,128)(2,1)S(1)}, bf16[32,8192]{1,0:T(8,128)(2,1)S(1)}, bf16[32,8192]{1,0:T(8,128)(2,1)S(1)}) custom-call(s32[142]{0:T(256)S(1)} %concatenate.18.info_ref, bf16[128,1024]{1,0:T(8,128)(2,1)S(1)} %get-tuple-element.41.turned_ref, bf16[128,256]{1,0:T(8,128)(2,1)S(1)} %get-tuple-element.42.kept_ref, ...), custom_call_target="tpu_custom_call" | custom-call | flops 4294967296 | bytes 2097152 | tf_op jit(solution)/shard_map/attend/pallas_call | solution.py:527
  199.3 1.3 collective-permute-start.23
  200.8 2.9 collective-permute-start.13
  203.8 29.1 %collective-permute-done.21 = bf16[64,8192]{1,0:T(8,128)(2,1)S(1)} collective-permute-done((bf16[64,8192]{1,0:T(8,128)(2,1)S(1)}, bf16[64,8192]{1,0:T(8,128)(2,1)S(1)}, u32[]{:S(2)}, u32[]{:S(2)}) %collective-permute-start.21) | collective-permute-done | bytes 1048608 | tf_op jit(solution)/shard_map/ppermute | solution.py:732
  232.9 4.4 %collective-permute-start.15 = (bf16[32,8192]{1,0:T(8,128)(2,1)S(1)}, bf16[32,8192]{1,0:T(8,128)(2,1)S(1)}, u32[]{:S(2)}, u32[]{:S(2)}) collective-permute-start(bf16[32,8192]{1,0:T(8,128)(2,1)S(1)} %get-tuple-element.45), channel_id=1, source_target_pairs={{0,1},{3,2},{4,5},{7,6},{8,9},{11,10},{12,13},{15,14},{16,17},{19,... | collective-permute-start | bytes 1572872 | tf_op jit(solution)/shard_map/ppermute | solution.py:734
  237.6 29.0 %collective-permute-done.13 = bf16[64,8192]{1,0:T(8,128)(2,1)S(1)} collective-permute-done((bf16[64,8192]{1,0:T(8,128)(2,1)S(1)}, bf16[64,8192]{1,0:T(8,128)(2,1)S(1)}, u32[]{:S(2)}, u32[]{:S(2)}) %collective-permute-start.13) | collective-permute-done | bytes 1048608 | tf_op jit(solution)/shard_map/ppermute | solution.py:732
  266.6 0.7 collective-permute-start.6
  268.5 1.3 collective-permute-start.8
  269.9 0.7 collective-permute-start.31
  270.6 45.5 %collective-permute-done.8 = bf16[32,8192]{1,0:T(8,128)(2,1)S(1)} collective-permute-done((bf16[32,8192]{1,0:T(8,128)(2,1)S(1)}, bf16[32,8192]{1,0:T(8,128)(2,1)S(1)}, u32[]{:S(2)}, u32[]{:S(2)}) %collective-permute-start.8) | collective-permute-done | bytes 524320 | tf_op jit(solution)/shard_map/ppermute | solution.py:736
  316.2 0.7 collective-permute-start.22
  317.2 0.7 collective-permute-start.14
  318.0 1.3 collective-permute-start.24
  319.5 1.3 collective-permute-start.34
  320.8 63.6 %collective-permute-done.24 = bf16[32,8192]{1,0:T(8,128)(2,1)S(1)} collective-permute-done((bf16[32,8192]{1,0:T(8,128)(2,1)S(1)}, bf16[32,8192]{1,0:T(8,128)(2,1)S(1)}, u32[]{:S(2)}, u32[]{:S(2)}) %collective-permute-start.24) | collective-permute-done | bytes 524320 | tf_op jit(solution)/shard_map/ppermute | solution.py:736
  384.4 1.3 collective-permute-start.16
  386.0 20.8 %collective-permute-done.16 = bf16[32,8192]{1,0:T(8,128)(2,1)S(1)} collective-permute-done((bf16[32,8192]{1,0:T(8,128)(2,1)S(1)}, bf16[32,8192]{1,0:T(8,128)(2,1)S(1)}, u32[]{:S(2)}, u32[]{:S(2)}) %collective-permute-start.16) | collective-permute-done | bytes 524320 | tf_op jit(solution)/shard_map/ppermute | solution.py:736
  407.3 1.4 collective-permute-done.25.refs_2_
  408.8 12.8 %collective-permute-done.17.refs_1_ = bf16[32,8192]{1,0:T(8,128)(2,1)S(1)} collective-permute-done((bf16[32,8192]{1,0:T(8,128)(2,1)S(1)}, bf16[32,8192]{1,0:T(8,128)(2,1)S(1)}, u32[]{:S(2)}, u32[]{:S(2)}) %collective-permute-start.17) | collective-permute-done | bytes 524320 | tf_op jit(solution)/shard_map/ppermute | solution.py:739
  421.5 1.9 finish.1
  (90 shorter events, 5.9 us)
Async XLA Ops:
  2.2 1.6 copy-start.3
  3.8 0.7 copy-start.8
  6.2 17.1 %copy-start.7 = (bf16[32,8192]{1,0:T(8,128)(2,1)}, bf16[32,8192]{1,0:T(8,128)(2,1)S(1)}, u32[]{:S(2)}) copy-start(bf16[32,8192]{1,0:T(8,128)(2,1)S(1)} %get-tuple-element.39.refs_0_) | copy-start | bytes 1572868
  6.2 38.4 %copy-start.6 = (bf16[32,8192]{1,0:T(8,128)(2,1)}, bf16[32,8192]{1,0:T(8,128)(2,1)S(1)}, u32[]{:S(2)}) copy-start(bf16[32,8192]{1,0:T(8,128)(2,1)S(1)} %get-tuple-element.46.refs_0_) | copy-start | bytes 1572868
  6.2 48.8 %copy-start.5 = (bf16[32,8192]{1,0:T(8,128)(2,1)}, bf16[32,8192]{1,0:T(8,128)(2,1)S(1)}, u32[]{:S(2)}) copy-start(bf16[32,8192]{1,0:T(8,128)(2,1)S(1)} %get-tuple-element.53.refs_0_) | copy-start | bytes 1572868
  6.2 15.9 %collective-permute-start.10 = (bf16[32,8192]{1,0:T(8,128)(2,1)S(1)}, bf16[32,8192]{1,0:T(8,128)(2,1)S(1)}, u32[]{:S(2)}, u32[]{:S(2)}) collective-permute-start(bf16[32,8192]{1,0:T(8,128)(2,1)S(1)} %get-tuple-element.39.refs_0_), channel_id=1, source_target_pairs={{0,1},{1,0},{2,3},{3,2},{4,5},{5,4},{6,7},{7,6},{8,9},{9,8},{10,11... | collective-permute-start | bytes 1572872 | tf_op jit(solution)/shard_map/ppermute | solution.py:669
  10.3 35.5 %copy-start.4 = (bf16[32,8192]{1,0:T(8,128)(2,1)}, bf16[32,8192]{1,0:T(8,128)(2,1)S(1)}, u32[]{:S(2)}) copy-start(bf16[32,8192]{1,0:T(8,128)(2,1)S(1)} %norm_some.2.refs_0_) | copy-start | bytes 1572868
  10.3 37.1 %collective-permute-start = (bf16[32,8192]{1,0:T(8,128)(2,1)S(1)}, bf16[32,8192]{1,0:T(8,128)(2,1)S(1)}, u32[]{:S(2)}, u32[]{:S(2)}) collective-permute-start(bf16[32,8192]{1,0:T(8,128)(2,1)S(1)} %norm_some.2.refs_0_), channel_id=1, source_target_pairs={{0,1},{1,0},{2,3},{3,2},{4,5},{5,4},{6,7},{7,6},{8,9},{9,8},{10,11... | collective-permute-start | bytes 1572872 | tf_op jit(solution)/shard_map/ppermute | solution.py:669
  10.3 51.4 %collective-permute-start.1 = (bf16[32,8192]{1,0:T(8,128)(2,1)S(1)}, bf16[32,8192]{1,0:T(8,128)(2,1)}, u32[]{:S(2)}, u32[]{:S(2)}) collective-permute-start(bf16[32,8192]{1,0:T(8,128)(2,1)S(1)} %norm_some.2.refs_0_), channel_id=1, source_target_pairs={{1,2},{2,1},{5,6},{6,5},{9,10},{10,9},{13,14},{14,13},{17,18},{18,... | collective-permute-start | bytes 1572872 | tf_op jit(solution)/shard_map/ppermute | solution.py:671
  11.8 32.8 %collective-permute-start.18 = (bf16[32,8192]{1,0:T(8,128)(2,1)S(1)}, bf16[32,8192]{1,0:T(8,128)(2,1)S(1)}, u32[]{:S(2)}, u32[]{:S(2)}) collective-permute-start(bf16[32,8192]{1,0:T(8,128)(2,1)S(1)} %get-tuple-element.46.refs_0_), channel_id=1, source_target_pairs={{0,1},{1,0},{2,3},{3,2},{4,5},{5,4},{6,7},{7,6},{8,9},{9,8},{10,11... | collective-permute-start | bytes 1572872 | tf_op jit(solution)/shard_map/ppermute | solution.py:669
  15.9 39.1 %collective-permute-start.26 = (bf16[32,8192]{1,0:T(8,128)(2,1)S(1)}, bf16[32,8192]{1,0:T(8,128)(2,1)S(1)}, u32[]{:S(2)}, u32[]{:S(2)}) collective-permute-start(bf16[32,8192]{1,0:T(8,128)(2,1)S(1)} %get-tuple-element.53.refs_0_), channel_id=1, source_target_pairs={{0,1},{1,0},{2,3},{3,2},{4,5},{5,4},{6,7},{7,6},{8,9},{9,8},{10,11... | collective-permute-start | bytes 1572872 | tf_op jit(solution)/shard_map/ppermute | solution.py:669
  22.1 34.0 %copy-start.10 = (bf16[32,8192]{1,0:T(8,128)(2,1)}, bf16[32,8192]{1,0:T(8,128)(2,1)S(1)}, u32[]{:S(2)}) copy-start(bf16[32,8192]{1,0:T(8,128)(2,1)S(1)} %collective-permute-done.10.refs_1_) | copy-start | bytes 1572868
  23.2 34.5 %copy-start.17 = (s32[4]{0:T(128)S(1)}, s32[4]{0:T(128)}, u32[]{:S(2)}) copy-start(s32[4]{0:T(128)} %param.19) | copy-start | bytes 52
  23.2 41.1 %copy-start.16 = (s32[4]{0:T(128)S(1)}, s32[4]{0:T(128)}, u32[]{:S(2)}) copy-start(s32[4]{0:T(128)} %param.17) | copy-start | bytes 52
  23.2 41.2 %collective-permute-start.11 = (bf16[64,8192]{1,0:T(8,128)(2,1)}, bf16[64,8192]{1,0:T(8,128)(2,1)}, u32[]{:S(2)}, u32[]{:S(2)}) collective-permute-start(bf16[64,8192]{1,0:T(8,128)(2,1)} %pad_maximum_fusion), channel_id=1, source_target_pairs={{1,2},{2,1},{5,6},{6,5},{9,10},{10,9},{13,14},{14,13},{17,18},{18,... | collective-permute-start | bytes 3145736 | tf_op jit(solution)/shard_map/ppermute | solution.py:690
  44.6 13.3 %copy-start.11 = (bf16[32,8192]{1,0:T(8,128)(2,1)}, bf16[32,8192]{1,0:T(8,128)(2,1)S(1)}, u32[]{:S(2)}) copy-start(bf16[32,8192]{1,0:T(8,128)(2,1)S(1)} %collective-permute-done.18.refs_1_) | copy-start | bytes 1572868
  45.7 20.1 %collective-permute-start.19 = (bf16[64,8192]{1,0:T(8,128)(2,1)}, bf16[64,8192]{1,0:T(8,128)(2,1)}, u32[]{:S(2)}, u32[]{:S(2)}) collective-permute-start(bf16[64,8192]{1,0:T(8,128)(2,1)} %pad_maximum_fusion.1), channel_id=1, source_target_pairs={{1,2},{2,1},{5,6},{6,5},{9,10},{10,9},{13,14},{14,13},{17,18},{18,... | collective-permute-start | bytes 3145736 | tf_op jit(solution)/shard_map/ppermute | solution.py:690
  47.4 26.5 %copy-start.13 = (bf16[32,8192]{1,0:T(8,128)(2,1)}, bf16[32,8192]{1,0:T(8,128)(2,1)S(1)}, u32[]{:S(2)}) copy-start(bf16[32,8192]{1,0:T(8,128)(2,1)S(1)} %collective-permute-done.refs_1_) | copy-start | bytes 1572868
  47.4 15.7 %collective-permute-start.2 = (bf16[32,8192]{1,0:T(8,128)(2,1)S(1)}, bf16[32,8192]{1,0:T(8,128)(2,1)S(1)}, u32[]{:S(2)}, u32[]{:S(2)}) collective-permute-start(bf16[32,8192]{1,0:T(8,128)(2,1)S(1)} %collective-permute-done.refs_1_), channel_id=1, source_target_pairs={{1,2},{2,1},{5,6},{6,5},{9,10},{10,9},{13,14},{14,13},{17,18},{18,... | collective-permute-start | bytes 1572872 | tf_op jit(solution)/shard_map/ppermute | solution.py:672
  55.0 18.9 %copy-start.9 = (bf16[32,8192]{1,0:T(8,128)(2,1)}, bf16[32,8192]{1,0:T(8,128)(2,1)S(1)}, u32[]{:S(2)}) copy-start(bf16[32,8192]{1,0:T(8,128)(2,1)S(1)} %collective-permute-done.26.refs_1_) | copy-start | bytes 1572868
  56.1 31.1 %collective-permute-start.27 = (bf16[64,8192]{1,0:T(8,128)(2,1)}, bf16[64,8192]{1,0:T(8,128)(2,1)}, u32[]{:S(2)}, u32[]{:S(2)}) collective-permute-start(bf16[64,8192]{1,0:T(8,128)(2,1)} %pad_maximum_fusion.2), channel_id=1, source_target_pairs={{1,2},{2,1},{5,6},{6,5},{9,10},{10,9},{13,14},{14,13},{17,18},{18,... | collective-permute-start | bytes 3145736 | tf_op jit(solution)/shard_map/ppermute | solution.py:690
  58.5 21.4 %all-to-all-start = ((s32[4,1,1]{2,1,0:T(1,128)}), s32[4,1,1]{2,1,0:T(1,128)S(1)}, u32[]{:S(2)}, u32[]{:S(2)}) async-start(s32[4,1,1]{2,1,0:T(1,128)} %copy.17), calls=%async_computation | async-start | bytes 4096 | tf_op jit(solution)/shard_map/all_to_all | solution.py:661
  61.8 27.0 %collective-permute-start.3 = (bf16[32,8192]{1,0:T(8,128)(2,1)}, bf16[32,8192]{1,0:T(8,128)(2,1)S(1)}, u32[]{:S(2)}, u32[]{:S(2)}) collective-permute-start(bf16[32,8192]{1,0:T(8,128)(2,1)} %collective-permute-done.1.refs_2_), channel_id=1, source_target_pairs={{1,0},{2,3},{5,4},{6,7},{9,8},{10,11},{13,12},{14,15},{17,16},{18,... | collective-permute-start | bytes 1572872 | tf_op jit(solution)/shard_map/ppermute | solution.py:673
  63.1 10.8 %copy-start.14 = (bf16[32,8192]{1,0:T(8,128)(2,1)}, bf16[32,8192]{1,0:T(8,128)(2,1)S(1)}, u32[]{:S(2)}) copy-start(bf16[32,8192]{1,0:T(8,128)(2,1)S(1)} %collective-permute-done.2.refs_3_) | copy-start | bytes 1572868
  63.1 38.2 %collective-permute-start.4 = (bf16[32,8192]{1,0:T(8,128)(2,1)S(1)}, bf16[32,8192]{1,0:T(8,128)(2,1)}, u32[]{:S(2)}, u32[]{:S(2)}) collective-permute-start(bf16[32,8192]{1,0:T(8,128)(2,1)S(1)} %collective-permute-done.2.refs_3_), channel_id=1, source_target_pairs={{1,0},{2,3},{5,4},{6,7},{9,8},{10,11},{13,12},{14,15},{17,16},{18,... | collective-permute-start | bytes 1572872 | tf_op jit(solution)/shard_map/ppermute | solution.py:674
  64.5 76.3 %collective-permute-start.12 = (bf16[64,8192]{1,0:T(8,128)(2,1)}, bf16[64,8192]{1,0:T(8,128)(2,1)}, u32[]{:S(2)}, u32[]{:S(2)}) collective-permute-start(bf16[64,8192]{1,0:T(8,128)(2,1)} %collective-permute-done.11.refs_2_), channel_id=1, source_target_pairs={{1,0},{2,3},{5,4},{6,7},{9,8},{10,11},{13,12},{14,15},{17,16},{18,... | collective-permute-start | bytes 3145736 | tf_op jit(solution)/shard_map/ppermute | solution.py:691
  65.8 88.4 %collective-permute-start.20 = (bf16[64,8192]{1,0:T(8,128)(2,1)}, bf16[64,8192]{1,0:T(8,128)(2,1)}, u32[]{:S(2)}, u32[]{:S(2)}) collective-permute-start(bf16[64,8192]{1,0:T(8,128)(2,1)} %collective-permute-done.19.refs_2_), channel_id=1, source_target_pairs={{1,0},{2,3},{5,4},{6,7},{9,8},{10,11},{13,12},{14,15},{17,16},{18,... | collective-permute-start | bytes 3145736 | tf_op jit(solution)/shard_map/ppermute | solution.py:691
  73.9 5.8 %copy-start = (bf16[1024,8192]{1,0:T(8,128)(2,1)}, bf16[1024,8192]{1,0:T(8,128)(2,1)S(1)}, u32[]{:S(2)}) copy-start(bf16[1024,8192]{1,0:T(8,128)(2,1)S(1)} %load.3.out_w_ref) | copy-start | bytes 50331652
  80.1 29.0 %slice-start = ((s8[16777216]{0:T(1024)(128)(4,1)}), s8[4194304]{0:T(1024)(128)(4,1)S(1)}, s32[]{:S(2)}) async-start(s8[16777216]{0:T(1024)(128)(4,1)} %bitcast.4), calls=%async_computation.1 | async-start | bytes 8388608
  80.1 29.0 %slice-start.1 = ((s8[16777216]{0:T(1024)(128)(4,1)}), s8[4194304]{0:T(1024)(128)(4,1)S(1)}, s32[]{:S(2)}) async-start(s8[16777216]{0:T(1024)(128)(4,1)} %bitcast.4), calls=%async_computation.2 | async-start | bytes 8388608
  87.2 21.9 %copy-start.1 = (bf16[8192,1024]{1,0:T(8,128)(2,1)}, bf16[8192,1024]{1,0:T(8,128)(2,1)S(1)}, u32[]{:S(2)}) copy-start(bf16[8192,1024]{1,0:T(8,128)(2,1)S(1)} %get-tuple-element.32.refs_6_.refs_4_) | copy-start | bytes 50331652
  87.2 75.0 %collective-permute-start.28 = (bf16[64,8192]{1,0:T(8,128)(2,1)}, bf16[64,8192]{1,0:T(8,128)(2,1)S(1)}, u32[]{:S(2)}, u32[]{:S(2)}) collective-permute-start(bf16[64,8192]{1,0:T(8,128)(2,1)} %collective-permute-done.27.refs_2_), channel_id=1, source_target_pairs={{1,0},{2,3},{5,4},{6,7},{9,8},{10,11},{13,12},{14,15},{17,16},{18,... | collective-permute-start | bytes 3145736 | tf_op jit(solution)/shard_map/ppermute | solution.py:691
  88.8 12.4 %copy-start.15 = (bf16[32,8192]{1,0:T(8,128)(2,1)}, bf16[32,8192]{1,0:T(8,128)(2,1)S(1)}, u32[]{:S(2)}) copy-start(bf16[32,8192]{1,0:T(8,128)(2,1)S(1)} %collective-permute-done.3.refs_4_) | copy-start | bytes 1572868
  101.2 7.9 %slice-start.2 = ((s8[16777216]{0:T(1024)(128)(4,1)}), s8[4194304]{0:T(1024)(128)(4,1)S(1)}, s32[]{:S(2)}) async-start(s8[16777216]{0:T(1024)(128)(4,1)} %bitcast.4), calls=%async_computation.3 | async-start | bytes 8388608
  101.3 7.9 %slice-start.3 = ((s8[16777216]{0:T(1024)(128)(4,1)}), s8[4194304]{0:T(1024)(128)(4,1)S(1)}, s32[]{:S(2)}) async-start(s8[16777216]{0:T(1024)(128)(4,1)} %bitcast.4), calls=%async_computation.4 | async-start | bytes 8388608
  118.3 72.1 %collective-permute-start.5 = (bf16[64,8192]{1,0:T(8,128)(2,1)S(1)}, bf16[64,8192]{1,0:T(8,128)(2,1)S(1)}, u32[]{:S(2)}, u32[]{:S(2)}) collective-permute-start(bf16[64,8192]{1,0:T(8,128)(2,1)S(1)} %get-tuple-element.37), channel_id=1, source_target_pairs={{0,1},{3,2},{4,5},{7,6},{8,9},{11,10},{12,13},{15,14},{16,17},{19,... | collective-permute-start | bytes 3145736 | tf_op jit(solution)/shard_map/ppermute | solution.py:732
  139.3 130.6 %collective-permute-start.7 = (bf16[32,8192]{1,0:T(8,128)(2,1)S(1)}, bf16[32,8192]{1,0:T(8,128)(2,1)S(1)}, u32[]{:S(2)}, u32[]{:S(2)}) collective-permute-start(bf16[32,8192]{1,0:T(8,128)(2,1)S(1)} %get-tuple-element.38), channel_id=1, source_target_pairs={{0,1},{3,2},{4,5},{7,6},{8,9},{11,10},{12,13},{15,14},{16,17},{19,... | collective-permute-start | bytes 1572872 | tf_op jit(solution)/shard_map/ppermute | solution.py:734
  140.8 5.8 %copy-start.2 = (bf16[8192,1024]{1,0:T(8,128)(2,1)S(1)}, bf16[8192,1024]{1,0:T(8,128)(2,1)}, u32[]{:S(2)}) copy-start(bf16[8192,1024]{1,0:T(8,128)(2,1)} %copy-done.1) | copy-start | bytes 50331652
  162.2 1.0 copy-start.12
  177.0 22.3 %collective-permute-start.32 = (bf16[32,8192]{1,0:T(8,128)(2,1)S(1)}, bf16[32,8192]{1,0:T(8,128)(2,1)S(1)}, u32[]{:S(2)}, u32[]{:S(2)}) collective-permute-start(bf16[32,8192]{1,0:T(8,128)(2,1)S(1)} %get-tuple-element.59), channel_id=1, source_target_pairs={{0,1},{3,2},{4,5},{7,6},{8,9},{11,10},{12,13},{15,14},{16,17},{19,... | collective-permute-start | bytes 1572872 | tf_op jit(solution)/shard_map/ppermute | solution.py:723
  178.6 22.2 %collective-permute-start.30 = (bf16[32,8192]{1,0:T(8,128)(2,1)S(1)}, bf16[32,8192]{1,0:T(8,128)(2,1)S(1)}, u32[]{:S(2)}, u32[]{:S(2)}) collective-permute-start(bf16[32,8192]{1,0:T(8,128)(2,1)S(1)} %get-tuple-element.60), channel_id=1, source_target_pairs={{0,1},{3,2},{4,5},{7,6},{8,9},{11,10},{12,13},{15,14},{16,17},{19,... | collective-permute-start | bytes 1572872 | tf_op jit(solution)/shard_map/ppermute | solution.py:724
  179.9 227.3 %collective-permute-start.29 = (bf16[32,8192]{1,0:T(8,128)(2,1)S(1)}, bf16[32,8192]{1,0:T(8,128)(2,1)S(1)}, u32[]{:S(2)}, u32[]{:S(2)}) collective-permute-start(bf16[32,8192]{1,0:T(8,128)(2,1)S(1)} %get-tuple-element.58), channel_id=1, source_target_pairs={{0,1},{3,2},{4,5},{7,6},{8,9},{11,10},{12,13},{15,14},{16,17},{19,... | collective-permute-start | bytes 1572872 | tf_op jit(solution)/shard_map/ppermute | solution.py:725
  190.4 42.5 %collective-permute-start.21 = (bf16[64,8192]{1,0:T(8,128)(2,1)S(1)}, bf16[64,8192]{1,0:T(8,128)(2,1)S(1)}, u32[]{:S(2)}, u32[]{:S(2)}) collective-permute-start(bf16[64,8192]{1,0:T(8,128)(2,1)S(1)} %get-tuple-element.51), channel_id=1, source_target_pairs={{0,1},{3,2},{4,5},{7,6},{8,9},{11,10},{12,13},{15,14},{16,17},{19,... | collective-permute-start | bytes 3145736 | tf_op jit(solution)/shard_map/ppermute | solution.py:732
  199.3 120.1 %collective-permute-start.23 = (bf16[32,8192]{1,0:T(8,128)(2,1)S(1)}, bf16[32,8192]{1,0:T(8,128)(2,1)S(1)}, u32[]{:S(2)}, u32[]{:S(2)}) collective-permute-start(bf16[32,8192]{1,0:T(8,128)(2,1)S(1)} %get-tuple-element.52), channel_id=1, source_target_pairs={{0,1},{3,2},{4,5},{7,6},{8,9},{11,10},{12,13},{15,14},{16,17},{19,... | collective-permute-start | bytes 1572872 | tf_op jit(solution)/shard_map/ppermute | solution.py:734
  200.8 65.8 %collective-permute-start.13 = (bf16[64,8192]{1,0:T(8,128)(2,1)S(1)}, bf16[64,8192]{1,0:T(8,128)(2,1)S(1)}, u32[]{:S(2)}, u32[]{:S(2)}) collective-permute-start(bf16[64,8192]{1,0:T(8,128)(2,1)S(1)} %get-tuple-element.44), channel_id=1, source_target_pairs={{0,1},{3,2},{4,5},{7,6},{8,9},{11,10},{12,13},{15,14},{16,17},{19,... | collective-permute-start | bytes 3145736 | tf_op jit(solution)/shard_map/ppermute | solution.py:732
  232.9 153.0 %collective-permute-start.15 = (bf16[32,8192]{1,0:T(8,128)(2,1)S(1)}, bf16[32,8192]{1,0:T(8,128)(2,1)S(1)}, u32[]{:S(2)}, u32[]{:S(2)}) collective-permute-start(bf16[32,8192]{1,0:T(8,128)(2,1)S(1)} %get-tuple-element.45), channel_id=1, source_target_pairs={{0,1},{3,2},{4,5},{7,6},{8,9},{11,10},{12,13},{15,14},{16,17},{19,... | collective-permute-start | bytes 1572872 | tf_op jit(solution)/shard_map/ppermute | solution.py:734
  266.6 1.0 collective-permute-start.6
  267.6 0.8 collective-permute-start.33
  268.5 47.7 %collective-permute-start.8 = (bf16[32,8192]{1,0:T(8,128)(2,1)S(1)}, bf16[32,8192]{1,0:T(8,128)(2,1)S(1)}, u32[]{:S(2)}, u32[]{:S(2)}) collective-permute-start(bf16[32,8192]{1,0:T(8,128)(2,1)S(1)} %add_convert_fusion.11), channel_id=1, source_target_pairs={{1,0},{2,3},{5,4},{6,7},{9,8},{10,11},{13,12},{14,15},{17,16},{18,... | collective-permute-start | bytes 1572872 | tf_op jit(solution)/shard_map/ppermute | solution.py:736
  269.9 137.4 %collective-permute-start.31 = (bf16[32,8192]{1,0:T(8,128)(2,1)S(1)}, bf16[32,8192]{1,0:T(8,128)(2,1)S(1)}, u32[]{:S(2)}, u32[]{:S(2)}) collective-permute-start(bf16[32,8192]{1,0:T(8,128)(2,1)S(1)} %add_convert_fusion.5), channel_id=1, source_target_pairs={{1,2},{2,1},{5,6},{6,5},{9,10},{10,9},{13,14},{14,13},{17,18},{18,... | collective-permute-start | bytes 1572872 | tf_op jit(solution)/shard_map/ppermute | solution.py:727
  316.2 1.0 collective-permute-start.22
  317.2 0.9 collective-permute-start.14
  318.0 66.3 %collective-permute-start.24 = (bf16[32,8192]{1,0:T(8,128)(2,1)S(1)}, bf16[32,8192]{1,0:T(8,128)(2,1)S(1)}, u32[]{:S(2)}, u32[]{:S(2)}) collective-permute-start(bf16[32,8192]{1,0:T(8,128)(2,1)S(1)} %add_convert_fusion.7), channel_id=1, source_target_pairs={{1,0},{2,3},{5,4},{6,7},{9,8},{10,11},{13,12},{14,15},{17,16},{18,... | collective-permute-start | bytes 1572872 | tf_op jit(solution)/shard_map/ppermute | solution.py:736
  319.5 87.8 %collective-permute-start.34 = (bf16[32,8192]{1,0:T(8,128)(2,1)S(1)}, bf16[32,8192]{1,0:T(8,128)(2,1)S(1)}, u32[]{:S(2)}, u32[]{:S(2)}) collective-permute-start(bf16[32,8192]{1,0:T(8,128)(2,1)S(1)} %add_convert_fusion.3), channel_id=1, source_target_pairs={{1,0},{2,3},{5,4},{6,7},{9,8},{10,11},{13,12},{14,15},{17,16},{18,... | collective-permute-start | bytes 1572872 | tf_op jit(solution)/shard_map/ppermute | solution.py:728
  384.4 22.5 %collective-permute-start.16 = (bf16[32,8192]{1,0:T(8,128)(2,1)S(1)}, bf16[32,8192]{1,0:T(8,128)(2,1)S(1)}, u32[]{:S(2)}, u32[]{:S(2)}) collective-permute-start(bf16[32,8192]{1,0:T(8,128)(2,1)S(1)} %add_convert_fusion.9), channel_id=1, source_target_pairs={{1,0},{2,3},{5,4},{6,7},{9,8},{10,11},{13,12},{14,15},{17,16},{18,... | collective-permute-start | bytes 1572872 | tf_op jit(solution)/shard_map/ppermute | solution.py:736
  385.9 21.4 %collective-permute-start.9 = (bf16[32,8192]{1,0:T(8,128)(2,1)S(1)}, bf16[32,8192]{1,0:T(8,128)(2,1)S(1)}, u32[]{:S(2)}, u32[]{:S(2)}) collective-permute-start(bf16[32,8192]{1,0:T(8,128)(2,1)S(1)} %add_convert_fusion.10), channel_id=1, source_target_pairs={{0,12},{4,8},{8,4},{12,0},{1,13},{5,9},{9,5},{13,1},{2,14},{6,10},... | collective-permute-start | bytes 1572872 | tf_op jit(solution)/shard_map/ppermute | solution.py:739
  406.8 1.9 collective-permute-start.25
  407.2 14.3 %collective-permute-start.17 = (bf16[32,8192]{1,0:T(8,128)(2,1)S(1)}, bf16[32,8192]{1,0:T(8,128)(2,1)S(1)}, u32[]{:S(2)}, u32[]{:S(2)}) collective-permute-start(bf16[32,8192]{1,0:T(8,128)(2,1)S(1)} %add_convert_fusion.8), channel_id=1, source_target_pairs={{0,8},{4,12},{8,0},{12,4},{1,9},{5,13},{9,1},{13,5},{2,10},{6,14},... | collective-permute-start | bytes 1572872 | tf_op jit(solution)/shard_map/ppermute | solution.py:739

commit v3 on v2

--- a/solution.py
+++ b/solution.py
@@ -220,7 +220,7 @@
 
 LINE = 4
 CHUNK = 128
-GROUP = 4
+GROUPS = (8, 4, 1)
 
 
 def pick_of(info_ref, turn, holding):
@@ -271,7 +271,7 @@
             transcendentals=rows,
         ),
         name="norm_some",
-    )(info, hidden, gain)
+    )(info, *stored_of(hidden), gain)
 
 
 def load_kernel(count, *refs):
@@ -411,7 +411,7 @@
 
 
 def stretch_kernel(
-    count, part, pieces, turn, holding, limit, length, group, tile, info_ref, turned_ref, kept_ref, cache_ref, out_w_ref, *refs
+    count, part, pieces, turn, holding, limit, length, tile, info_ref, turned_ref, kept_ref, cache_ref, out_w_ref, *refs
 ):
     outs = refs[:count]
     stored, product, heads_ref, top_ref, sum_ref, acc_ref, page_sems, out_sems = refs[count:]
@@ -437,27 +437,43 @@
         page_copy(place).start()
 
     def fold(keys, values, mask):
-        for first in range(0, lanes, chunk):
+        def score(first):
+            return jnp.dot(keys, turned_ref[:, first : first + chunk], preferred_element_type=jnp.float32)
+
+        firsts = list(range(0, lanes, chunk))
+        coming = score(0)
+        flipped = values.T
+        waiting = None
+
+        def settle(first, exps, summed, fade):
             span = slice(first, first + chunk)
-            scores = jnp.dot(keys, turned_ref[:, span], preferred_element_type=jnp.float32)
-            if mask is not None:
-                scores = jnp.where(mask, scores, MASKED)
-                top = jnp.max(scores, axis=0, keepdims=True)
-            else:
-                top = jnp.maximum(top_ref[:, span], jnp.max(scores, axis=0, keepdims=True))
-            exps = jnp.exp2((scores - top) * scale)
-            summed = jnp.sum(exps, axis=0, keepdims=True)
-            taken = lax.dot_general(
-                values, exps.astype(jnp.bfloat16), (((0,), (0,)), ((), ())), preferred_element_type=jnp.float32
-            )
+            taken = jnp.dot(flipped, exps, preferred_element_type=jnp.float32)
             if mask is not None:
                 sum_ref[:, span] = summed
                 acc_ref[:, span] = taken
             else:
-                fade = jnp.exp2((top_ref[:, span] - top) * scale)
                 sum_ref[:, span] = sum_ref[:, span] * fade + summed
                 acc_ref[:, span] = acc_ref[:, span] * fade + taken
+
+        for place, first in enumerate(firsts):
+            span = slice(first, first + chunk)
+            scores = coming
+            if place + 1 < len(firsts):
+                coming = score(firsts[place + 1])
+            if mask is not None:
+                scores = jnp.where(mask, scores, MASKED)
+                top = jnp.max(scores, axis=0, keepdims=True)
+                fade = None
+            else:
+                old = top_ref[:, span]
+                top = jnp.maximum(old, jnp.max(scores, axis=0, keepdims=True))
+                fade = jnp.exp2((old - top) * scale)
+            exps = jnp.exp2((scores - top) * scale)
             top_ref[:, span] = top
+            if waiting is not None:
+                settle(*waiting)
+            waiting = (first, exps.astype(jnp.bfloat16), jnp.sum(exps, axis=0, keepdims=True), fade)
+        settle(*waiting)
 
     chunk = min(lanes, CHUNK)
     key_row = lax.broadcasted_iota(jnp.int32, (length, chunk), 0)
@@ -470,15 +486,16 @@
         rows = pl.ds(pl.multiple_of(first * block, block), span * block)
         fold(stored[rows, :head_width], stored[rows, head_width:], None)
 
-    whole = pages // group
-
-    @pl.loop(0, whole)
-    def _(step):
-        fold_span(step * group, group)
-
-    @pl.loop(whole * group, pages)
-    def _(place):
-        fold_span(place, 1)
+    done = 0
+    for span in GROUPS:
+        span = min(span, limit)
+        until = pages // span
+
+        @pl.loop(done // span, until)
+        def _(step):
+            fold_span(step * span, span)
+
+        done = until * span
 
     share = acc_ref[...] / sum_ref[...]
     row = lax.broadcasted_iota(jnp.int32, (length, head_width), 0)
@@ -523,10 +540,9 @@
     inner, width = w_out.shape
     tile = min(width, 1024)
     tiles = width // tile
-    group = min(GROUP, limit)
     return pl.pallas_call(
         functools.partial(
-            stretch_kernel, len(sizes), part, pieces, turn, holding, limit, length, group, tile
+            stretch_kernel, len(sizes), part, pieces, turn, holding, limit, length, tile
         ),
         grid_spec=pltpu.PrefetchScalarGridSpec(
             num_scalar_prefetch=1,

time: 425 us -> 432 us (1.016)
    ppermute x3, waiting for transfers between devices: 130 us -> 135 us  [paired(): from_inner = lax.ppermute(outgoing, 'tp', outward)]
    unnamed x44 -> x42, local copies, waits for them, and re-layouts: 14.9 us -> 13.3 us
where the time goes in v3:
time: 432 us; the launch traced here: 430 us
  waiting for transfers between devices  252 us (58%)
  Pallas kernels  82.5 us (19%)
  starting transfers between devices  71.1 us (16%)
  local copies, waits for them, and re-layouts  15.5 us (4%)
  other arithmetic  7.23 us (2%)
    ppermute x3, waiting for transfers between devices, paired(): from_inner = lax.ppermute(outgoing, 'tp', outward)  135 us
    ppermute x3, waiting for transfers between devices, paired(): joined = lax.ppermute(far_part, 'tp', inward)  58.2 us
    pallas_call x4, Pallas kernels, attend_stretch(): pl.pallas_call(functools.partial(stretch_kernel, len(sizes), part, pieces...  31.9 us
    ppermute x4, waiting for transfers between devices, paired(): sibling = lax.ppermute(own, 'tp', sides)  31.5 us
    pallas_call x4, Pallas kernels, project(): pl.pallas_call(functools.partial(project_kernel, len(sources), share, pla...  30.5 us
    ppermute x3, starting transfers between devices, paired(): joined = lax.ppermute(far_part, 'tp', inward)  26.2 us
    ppermute x3, waiting for transfers between devices, paired(): arrived.append(lax.ppermute(branch, 'dp', pairs))  14.3 us
    unnamed x42, local copies, waits for them, and re-layouts  13.3 us
  transfers between devices with their start and end apart: 36, of which 12 were waited for; matrix products, arithmetic and copies ran while one was open for 2% of the time, Pallas kernels for 18%

profile of v3, /device:TPU:0, one launch (start us, length us, event | category | flops | bytes accessed | tf_op | source)
XLA Modules:
  0.0 430.4 jit_solution(1104813238483993619)
XLA Ops:
  0.6 0.8 reshape.41
  1.4 0.8 concatenate.18.info_ref
  2.2 0.7 copy-done.7
  2.9 3.4 norm_some.3
  6.3 3.1 collective-permute-start.10
  9.5 1.9 norm_some.2.refs_0_
  11.5 1.5 collective-permute-start.1
  13.0 4.1 collective-permute-start.18
  17.1 5.1 %collective-permute-done.10.refs_1_ = bf16[32,8192]{1,0:T(8,128)(2,1)S(1)} collective-permute-done((bf16[32,8192]{1,0:T(8,128)(2,1)S(1)}, bf16[32,8192]{1,0:T(8,128)(2,1)S(1)}, u32[]{:S(2)}, u32[]{:S(2)}) %collective-permute-start.10) | collective-permute-done | bytes 524320 | tf_op jit(solution)/shard_map/ppermute | solution.py:685
  22.2 1.1 pad_maximum_fusion
  23.3 1.8 collective-permute-start.11
  25.2 19.5 %collective-permute-done.18.refs_1_ = bf16[32,8192]{1,0:T(8,128)(2,1)S(1)} collective-permute-done((bf16[32,8192]{1,0:T(8,128)(2,1)S(1)}, bf16[32,8192]{1,0:T(8,128)(2,1)S(1)}, u32[]{:S(2)}, u32[]{:S(2)}) %collective-permute-start.18) | collective-permute-done | bytes 524320 | tf_op jit(solution)/shard_map/ppermute | solution.py:685
  44.7 1.2 pad_maximum_fusion.1
  45.9 1.7 collective-permute-start.19
  48.2 6.8 %collective-permute-done.26.refs_1_ = bf16[32,8192]{1,0:T(8,128)(2,1)S(1)} collective-permute-done((bf16[32,8192]{1,0:T(8,128)(2,1)S(1)}, bf16[32,8192]{1,0:T(8,128)(2,1)S(1)}, u32[]{:S(2)}, u32[]{:S(2)}) %collective-permute-start.26) | collective-permute-done | bytes 524320 | tf_op jit(solution)/shard_map/ppermute | solution.py:685
  55.1 1.1 pad_maximum_fusion.2
  56.2 1.6 collective-permute-start.27
  58.7 3.2 all-to-all-start
  61.9 1.3 collective-permute-start.3
  63.2 1.3 collective-permute-start.4
  64.6 1.3 collective-permute-start.12
  65.9 1.3 collective-permute-start.20
  67.2 1.0 fusion
  68.2 5.8 %load.3.out_w_ref = bf16[1024,8192]{1,0:T(8,128)(2,1)S(1)} custom-call(bf16[1024,8192]{1,0:T(8,128)(2,1)} %refs_0_.3), custom_call_target="tpu_custom_call" | custom-call | tf_op jit(solution)/shard_map/load/pallas_call | solution.py:290
  74.0 5.8 %copy-done = bf16[1024,8192]{1,0:T(8,128)(2,1)} copy-done((bf16[1024,8192]{1,0:T(8,128)(2,1)}, bf16[1024,8192]{1,0:T(8,128)(2,1)S(1)}, u32[]{:S(2)}) %copy-start) | copy-done | bytes 16777240
  80.2 7.1 %load.2 = (bf16[8192,1024]{1,0:T(8,128)(2,1)S(1)}, bf16[8192,256]{1,0:T(8,128)(2,1)S(1)}) custom-call(bf16[8192,1024]{1,0:T(8,128)(2,1)} %refs_0_.2, bf16[8192,256]{1,0:T(8,128)(2,1)} %refs_1_.1, s32[4]{0:T(128)S(1)} %reduce.refs_2_.labels_ref), custom_call_target="tpu_custom_call" | custom-call | tf_op jit(solution)/shard_map/load/pallas_call | solution.py:290
  87.4 1.6 collective-permute-start.28
  89.0 12.4 %collective-permute-done.4.refs_5_ = bf16[32,8192]{1,0:T(8,128)(2,1)} collective-permute-done((bf16[32,8192]{1,0:T(8,128)(2,1)S(1)}, bf16[32,8192]{1,0:T(8,128)(2,1)}, u32[]{:S(2)}, u32[]{:S(2)}) %collective-permute-start.4) | collective-permute-done | bytes 524320 | tf_op jit(solution)/shard_map/ppermute | solution.py:690
  101.4 7.8 %project.4 = (bf16[128,1024]{1,0:T(8,128)(2,1)S(1)}, bf16[128,256]{1,0:T(8,128)(2,1)S(1)}, bf16[4,128,256]{2,1,0:T(8,128)(2,1)}) custom-call(s32[142]{0:T(256)S(1)} %concatenate.18.info_ref, bf16[32,8192]{1,0:T(8,128)(2,1)} %copy-done.3, bf16[32,8192]{1,0:T(8,128)(2,1)} %copy-done.12, bf16[32,8192]{1,0:T(8,128)(2,1)} %collective-permute-done.1.refs_2_, ...), custom_call_target="tpu_custom_call" | custom-call | flops 2684354560 | bytes 2097152 | tf_op jit(solution)/shard_map/project/pallas_call | solution.py:376
  109.3 9.1 %attend.4 = (bf16[64,8192]{1,0:T(8,128)(2,1)S(1)}, bf16[32,8192]{1,0:T(8,128)(2,1)S(1)}, bf16[32,8192]{1,0:T(8,128)(2,1)S(1)}) custom-call(s32[142]{0:T(256)S(1)} %concatenate.18.info_ref, bf16[128,1024]{1,0:T(8,128)(2,1)S(1)} %get-tuple-element.34.turned_ref, bf16[128,256]{1,0:T(8,128)(2,1)S(1)} %get-tuple-element.35.kept_ref, ...), custom_call_target="tpu_custom_call" | custom-call | flops 4294967296 | bytes 2097152 | tf_op jit(solution)/shard_map/attend/pallas_call | solution.py:543
  118.4 21.0 %collective-permute-start.5 = (bf16[64,8192]{1,0:T(8,128)(2,1)S(1)}, bf16[64,8192]{1,0:T(8,128)(2,1)S(1)}, u32[]{:S(2)}, u32[]{:S(2)}) collective-permute-start(bf16[64,8192]{1,0:T(8,128)(2,1)S(1)} %get-tuple-element.37), channel_id=1, source_target_pairs={{0,1},{3,2},{4,5},{7,6},{8,9},{11,10},{12,13},{15,14},{16,17},{19,... | collective-permute-start | bytes 3145736 | tf_op jit(solution)/shard_map/ppermute | solution.py:748
  139.5 1.5 collective-permute-start.7
  141.0 5.8 %copy-done.2 = bf16[8192,1024]{1,0:T(8,128)(2,1)S(1)} copy-done((bf16[8192,1024]{1,0:T(8,128)(2,1)S(1)}, bf16[8192,1024]{1,0:T(8,128)(2,1)}, u32[]{:S(2)}) %copy-start.2) | copy-done | bytes 16777240
  146.8 7.6 %project.5 = (bf16[128,1024]{1,0:T(8,128)(2,1)S(1)}, bf16[128,256]{1,0:T(8,128)(2,1)S(1)}, bf16[4,128,256]{2,1,0:T(8,128)(2,1)}) custom-call(s32[142]{0:T(256)S(1)} %concatenate.18.info_ref, bf16[32,8192]{1,0:T(8,128)(2,1)} %copy-done.6, bf16[32,8192]{1,0:T(8,128)(2,1)} %copy-done.9, ...), custom_call_target="tpu_custom_call", output_to_operand_aliasing={{2}: (9, {})} | custom-call | flops 2684354560 | bytes 2097152 | tf_op jit(solution)/shard_map/project/pallas_call | solution.py:376
  154.3 7.6 %project.6 = (bf16[128,1024]{1,0:T(8,128)(2,1)S(1)}, bf16[128,256]{1,0:T(8,128)(2,1)S(1)}, bf16[4,128,256]{2,1,0:T(8,128)(2,1)}) custom-call(s32[142]{0:T(256)S(1)} %concatenate.18.info_ref, bf16[32,8192]{1,0:T(8,128)(2,1)} %copy-done.5, bf16[32,8192]{1,0:T(8,128)(2,1)} %copy-done.10, ...), custom_call_target="tpu_custom_call", output_to_operand_aliasing={{2}: (9, {})} | custom-call | flops 2684354560 | bytes 2097152 | tf_op jit(solution)/shard_map/project/pallas_call | solution.py:376
  161.9 1.1 collective-permute-done.28.refs_3_
  163.0 1.0 copy-done.11
  164.0 7.5 %project.7 = (bf16[128,1024]{1,0:T(8,128)(2,1)S(1)}, bf16[128,256]{1,0:T(8,128)(2,1)S(1)}, bf16[4,128,256]{2,1,0:T(8,128)(2,1)}) custom-call(s32[142]{0:T(256)S(1)} %concatenate.18.info_ref, bf16[32,8192]{1,0:T(8,128)(2,1)} %copy-done.4, bf16[32,8192]{1,0:T(8,128)(2,1)} %copy-done.8, ...), custom_call_target="tpu_custom_call", output_to_operand_aliasing={{2}: (9, {})} | custom-call | flops 2684354560 | bytes 2097152 | tf_op jit(solution)/shard_map/project/pallas_call | solution.py:376
  171.5 6.3 %attend.7 = (bf16[32,8192]{1,0:T(8,128)(2,1)S(1)}, bf16[32,8192]{1,0:T(8,128)(2,1)S(1)}, bf16[32,8192]{1,0:T(8,128)(2,1)S(1)}, bf16[32,8192]{1,0:T(8,128)(2,1)S(1)}) custom-call(s32[142]{0:T(256)S(1)} %concatenate.18.info_ref, bf16[128,1024]{1,0:T(8,128)(2,1)S(1)} %get-tuple-element.55.turned_ref, bf16[128,256]{1,0:T(8,128)(2,1)S(1)} %get-tuple-element.56.kept_ref, ...), custom_call_target="tpu_custom_call" | custom-call | flops 4294967296 | bytes 2097152 | tf_op jit(solution)/shard_map/attend/pallas_call | solution.py:543
  177.8 1.6 collective-permute-start.32
  179.4 1.3 collective-permute-start.30
  180.7 1.3 collective-permute-start.29
  182.0 9.4 %attend.6 = (bf16[64,8192]{1,0:T(8,128)(2,1)S(1)}, bf16[32,8192]{1,0:T(8,128)(2,1)S(1)}, bf16[32,8192]{1,0:T(8,128)(2,1)S(1)}) custom-call(s32[142]{0:T(256)S(1)} %concatenate.18.info_ref, bf16[128,1024]{1,0:T(8,128)(2,1)S(1)} %get-tuple-element.48.turned_ref, bf16[128,256]{1,0:T(8,128)(2,1)S(1)} %get-tuple-element.49.kept_ref, ...), custom_call_target="tpu_custom_call" | custom-call | flops 4294967296 | bytes 2097152 | tf_op jit(solution)/shard_map/attend/pallas_call | solution.py:543
  191.4 1.4 collective-permute-start.21
  193.0 7.1 %attend.5 = (bf16[64,8192]{1,0:T(8,128)(2,1)S(1)}, bf16[32,8192]{1,0:T(8,128)(2,1)S(1)}, bf16[32,8192]{1,0:T(8,128)(2,1)S(1)}) custom-call(s32[142]{0:T(256)S(1)} %concatenate.18.info_ref, bf16[128,1024]{1,0:T(8,128)(2,1)S(1)} %get-tuple-element.41.turned_ref, bf16[128,256]{1,0:T(8,128)(2,1)S(1)} %get-tuple-element.42.kept_ref, ...), custom_call_target="tpu_custom_call" | custom-call | flops 4294967296 | bytes 2097152 | tf_op jit(solution)/shard_map/attend/pallas_call | solution.py:543
  200.1 1.3 collective-permute-start.23
  201.6 3.8 collective-permute-start.13
  205.6 29.1 %collective-permute-done.21 = bf16[64,8192]{1,0:T(8,128)(2,1)S(1)} collective-permute-done((bf16[64,8192]{1,0:T(8,128)(2,1)S(1)}, bf16[64,8192]{1,0:T(8,128)(2,1)S(1)}, u32[]{:S(2)}, u32[]{:S(2)}) %collective-permute-start.21) | collective-permute-done | bytes 1048608 | tf_op jit(solution)/shard_map/ppermute | solution.py:748
  234.7 4.4 %collective-permute-start.15 = (bf16[32,8192]{1,0:T(8,128)(2,1)S(1)}, bf16[32,8192]{1,0:T(8,128)(2,1)S(1)}, u32[]{:S(2)}, u32[]{:S(2)}) collective-permute-start(bf16[32,8192]{1,0:T(8,128)(2,1)S(1)} %get-tuple-element.45), channel_id=1, source_target_pairs={{0,1},{3,2},{4,5},{7,6},{8,9},{11,10},{12,13},{15,14},{16,17},{19,... | collective-permute-start | bytes 1572872 | tf_op jit(solution)/shard_map/ppermute | solution.py:750
  239.4 29.0 %collective-permute-done.13 = bf16[64,8192]{1,0:T(8,128)(2,1)S(1)} collective-permute-done((bf16[64,8192]{1,0:T(8,128)(2,1)S(1)}, bf16[64,8192]{1,0:T(8,128)(2,1)S(1)}, u32[]{:S(2)}, u32[]{:S(2)}) %collective-permute-start.13) | collective-permute-done | bytes 1048608 | tf_op jit(solution)/shard_map/ppermute | solution.py:748
  268.4 0.7 collective-permute-start.6
  269.4 0.7 collective-permute-start.33
  270.3 1.3 collective-permute-start.8
  272.4 51.6 %collective-permute-done.8 = bf16[32,8192]{1,0:T(8,128)(2,1)S(1)} collective-permute-done((bf16[32,8192]{1,0:T(8,128)(2,1)S(1)}, bf16[32,8192]{1,0:T(8,128)(2,1)S(1)}, u32[]{:S(2)}, u32[]{:S(2)}) %collective-permute-start.8) | collective-permute-done | bytes 524320 | tf_op jit(solution)/shard_map/ppermute | solution.py:752
  324.0 0.7 collective-permute-start.22
  325.0 0.7 collective-permute-start.14
  325.9 1.3 collective-permute-start.24
  327.3 1.3 collective-permute-start.34
  328.6 63.9 %collective-permute-done.24 = bf16[32,8192]{1,0:T(8,128)(2,1)S(1)} collective-permute-done((bf16[32,8192]{1,0:T(8,128)(2,1)S(1)}, bf16[32,8192]{1,0:T(8,128)(2,1)S(1)}, u32[]{:S(2)}, u32[]{:S(2)}) %collective-permute-start.24) | collective-permute-done | bytes 524320 | tf_op jit(solution)/shard_map/ppermute | solution.py:752
  392.6 1.3 collective-permute-start.16
  394.2 19.4 %collective-permute-done.16 = bf16[32,8192]{1,0:T(8,128)(2,1)S(1)} collective-permute-done((bf16[32,8192]{1,0:T(8,128)(2,1)S(1)}, bf16[32,8192]{1,0:T(8,128)(2,1)S(1)}, u32[]{:S(2)}, u32[]{:S(2)}) %collective-permute-start.16) | collective-permute-done | bytes 524320 | tf_op jit(solution)/shard_map/ppermute | solution.py:752
  414.0 1.5 collective-permute-done.25.refs_2_
  415.5 12.8 %collective-permute-done.17.refs_1_ = bf16[32,8192]{1,0:T(8,128)(2,1)S(1)} collective-permute-done((bf16[32,8192]{1,0:T(8,128)(2,1)S(1)}, bf16[32,8192]{1,0:T(8,128)(2,1)S(1)}, u32[]{:S(2)}, u32[]{:S(2)}) %collective-permute-start.17) | collective-permute-done | bytes 524320 | tf_op jit(solution)/shard_map/ppermute | solution.py:755
  428.3 1.9 finish.1
  (88 shorter events, 5.3 us)
Async XLA Ops:
  2.2 0.7 copy-start.7
  6.3 17.0 %copy-start.6 = (bf16[32,8192]{1,0:T(8,128)(2,1)}, bf16[32,8192]{1,0:T(8,128)(2,1)S(1)}, u32[]{:S(2)}) copy-start(bf16[32,8192]{1,0:T(8,128)(2,1)S(1)} %get-tuple-element.39.refs_0_) | copy-start | bytes 1572868
  6.3 38.4 %copy-start.5 = (bf16[32,8192]{1,0:T(8,128)(2,1)}, bf16[32,8192]{1,0:T(8,128)(2,1)S(1)}, u32[]{:S(2)}) copy-start(bf16[32,8192]{1,0:T(8,128)(2,1)S(1)} %get-tuple-element.46.refs_0_) | copy-start | bytes 1572868
  6.3 48.8 %copy-start.4 = (bf16[32,8192]{1,0:T(8,128)(2,1)}, bf16[32,8192]{1,0:T(8,128)(2,1)S(1)}, u32[]{:S(2)}) copy-start(bf16[32,8192]{1,0:T(8,128)(2,1)S(1)} %get-tuple-element.53.refs_0_) | copy-start | bytes 1572868
  6.3 15.9 %collective-permute-start.10 = (bf16[32,8192]{1,0:T(8,128)(2,1)S(1)}, bf16[32,8192]{1,0:T(8,128)(2,1)S(1)}, u32[]{:S(2)}, u32[]{:S(2)}) collective-permute-start(bf16[32,8192]{1,0:T(8,128)(2,1)S(1)} %get-tuple-element.39.refs_0_), channel_id=1, source_target_pairs={{0,1},{1,0},{2,3},{3,2},{4,5},{5,4},{6,7},{7,6},{8,9},{9,8},{10,11... | collective-permute-start | bytes 1572872 | tf_op jit(solution)/shard_map/ppermute | solution.py:685
  11.4 34.4 %copy-start.3 = (bf16[32,8192]{1,0:T(8,128)(2,1)}, bf16[32,8192]{1,0:T(8,128)(2,1)S(1)}, u32[]{:S(2)}) copy-start(bf16[32,8192]{1,0:T(8,128)(2,1)S(1)} %norm_some.2.refs_0_) | copy-start | bytes 1572868
  11.4 36.1 %collective-permute-start = (bf16[32,8192]{1,0:T(8,128)(2,1)S(1)}, bf16[32,8192]{1,0:T(8,128)(2,1)S(1)}, u32[]{:S(2)}, u32[]{:S(2)}) collective-permute-start(bf16[32,8192]{1,0:T(8,128)(2,1)S(1)} %norm_some.2.refs_0_), channel_id=1, source_target_pairs={{0,1},{1,0},{2,3},{3,2},{4,5},{5,4},{6,7},{7,6},{8,9},{9,8},{10,11... | collective-permute-start | bytes 1572872 | tf_op jit(solution)/shard_map/ppermute | solution.py:685
  11.5 50.4 %collective-permute-start.1 = (bf16[32,8192]{1,0:T(8,128)(2,1)S(1)}, bf16[32,8192]{1,0:T(8,128)(2,1)}, u32[]{:S(2)}, u32[]{:S(2)}) collective-permute-start(bf16[32,8192]{1,0:T(8,128)(2,1)S(1)} %norm_some.2.refs_0_), channel_id=1, source_target_pairs={{1,2},{2,1},{5,6},{6,5},{9,10},{10,9},{13,14},{14,13},{17,18},{18,... | collective-permute-start | bytes 1572872 | tf_op jit(solution)/shard_map/ppermute | solution.py:687
  13.0 31.7 %collective-permute-start.18 = (bf16[32,8192]{1,0:T(8,128)(2,1)S(1)}, bf16[32,8192]{1,0:T(8,128)(2,1)S(1)}, u32[]{:S(2)}, u32[]{:S(2)}) collective-permute-start(bf16[32,8192]{1,0:T(8,128)(2,1)S(1)} %get-tuple-element.46.refs_0_), channel_id=1, source_target_pairs={{0,1},{1,0},{2,3},{3,2},{4,5},{5,4},{6,7},{7,6},{8,9},{9,8},{10,11... | collective-permute-start | bytes 1572872 | tf_op jit(solution)/shard_map/ppermute | solution.py:685
  17.1 38.0 %collective-permute-start.26 = (bf16[32,8192]{1,0:T(8,128)(2,1)S(1)}, bf16[32,8192]{1,0:T(8,128)(2,1)S(1)}, u32[]{:S(2)}, u32[]{:S(2)}) collective-permute-start(bf16[32,8192]{1,0:T(8,128)(2,1)S(1)} %get-tuple-element.53.refs_0_), channel_id=1, source_target_pairs={{0,1},{1,0},{2,3},{3,2},{4,5},{5,4},{6,7},{7,6},{8,9},{9,8},{10,11... | collective-permute-start | bytes 1572872 | tf_op jit(solution)/shard_map/ppermute | solution.py:685
  22.2 34.0 %copy-start.9 = (bf16[32,8192]{1,0:T(8,128)(2,1)}, bf16[32,8192]{1,0:T(8,128)(2,1)S(1)}, u32[]{:S(2)}) copy-start(bf16[32,8192]{1,0:T(8,128)(2,1)S(1)} %collective-permute-done.10.refs_1_) | copy-start | bytes 1572868
  23.3 34.5 %copy-start.16 = (s32[4]{0:T(128)S(1)}, s32[4]{0:T(128)}, u32[]{:S(2)}) copy-start(s32[4]{0:T(128)} %param.19) | copy-start | bytes 52
  23.3 41.2 %copy-start.15 = (s32[4]{0:T(128)S(1)}, s32[4]{0:T(128)}, u32[]{:S(2)}) copy-start(s32[4]{0:T(128)} %param.17) | copy-start | bytes 52
  23.3 41.3 %collective-permute-start.11 = (bf16[64,8192]{1,0:T(8,128)(2,1)}, bf16[64,8192]{1,0:T(8,128)(2,1)}, u32[]{:S(2)}, u32[]{:S(2)}) collective-permute-start(bf16[64,8192]{1,0:T(8,128)(2,1)} %pad_maximum_fusion), channel_id=1, source_target_pairs={{1,2},{2,1},{5,6},{6,5},{9,10},{10,9},{13,14},{14,13},{17,18},{18,... | collective-permute-start | bytes 3145736 | tf_op jit(solution)/shard_map/ppermute | solution.py:706
  44.7 13.3 %copy-start.10 = (bf16[32,8192]{1,0:T(8,128)(2,1)}, bf16[32,8192]{1,0:T(8,128)(2,1)S(1)}, u32[]{:S(2)}) copy-start(bf16[32,8192]{1,0:T(8,128)(2,1)S(1)} %collective-permute-done.18.refs_1_) | copy-start | bytes 1572868
  45.9 20.1 %collective-permute-start.19 = (bf16[64,8192]{1,0:T(8,128)(2,1)}, bf16[64,8192]{1,0:T(8,128)(2,1)}, u32[]{:S(2)}, u32[]{:S(2)}) collective-permute-start(bf16[64,8192]{1,0:T(8,128)(2,1)} %pad_maximum_fusion.1), channel_id=1, source_target_pairs={{1,2},{2,1},{5,6},{6,5},{9,10},{10,9},{13,14},{14,13},{17,18},{18,... | collective-permute-start | bytes 3145736 | tf_op jit(solution)/shard_map/ppermute | solution.py:706
  47.5 26.5 %copy-start.12 = (bf16[32,8192]{1,0:T(8,128)(2,1)}, bf16[32,8192]{1,0:T(8,128)(2,1)S(1)}, u32[]{:S(2)}) copy-start(bf16[32,8192]{1,0:T(8,128)(2,1)S(1)} %collective-permute-done.refs_1_) | copy-start | bytes 1572868
  47.5 15.7 %collective-permute-start.2 = (bf16[32,8192]{1,0:T(8,128)(2,1)S(1)}, bf16[32,8192]{1,0:T(8,128)(2,1)S(1)}, u32[]{:S(2)}, u32[]{:S(2)}) collective-permute-start(bf16[32,8192]{1,0:T(8,128)(2,1)S(1)} %collective-permute-done.refs_1_), channel_id=1, source_target_pairs={{1,2},{2,1},{5,6},{6,5},{9,10},{10,9},{13,14},{14,13},{17,18},{18,... | collective-permute-start | bytes 1572872 | tf_op jit(solution)/shard_map/ppermute | solution.py:688
  55.1 18.9 %copy-start.8 = (bf16[32,8192]{1,0:T(8,128)(2,1)}, bf16[32,8192]{1,0:T(8,128)(2,1)S(1)}, u32[]{:S(2)}) copy-start(bf16[32,8192]{1,0:T(8,128)(2,1)S(1)} %collective-permute-done.26.refs_1_) | copy-start | bytes 1572868
  56.2 31.1 %collective-permute-start.27 = (bf16[64,8192]{1,0:T(8,128)(2,1)}, bf16[64,8192]{1,0:T(8,128)(2,1)}, u32[]{:S(2)}, u32[]{:S(2)}) collective-permute-start(bf16[64,8192]{1,0:T(8,128)(2,1)} %pad_maximum_fusion.2), channel_id=1, source_target_pairs={{1,2},{2,1},{5,6},{6,5},{9,10},{10,9},{13,14},{14,13},{17,18},{18,... | collective-permute-start | bytes 3145736 | tf_op jit(solution)/shard_map/ppermute | solution.py:706
  58.7 21.4 %all-to-all-start = ((s32[4,1,1]{2,1,0:T(1,128)}), s32[4,1,1]{2,1,0:T(1,128)S(1)}, u32[]{:S(2)}, u32[]{:S(2)}) async-start(s32[4,1,1]{2,1,0:T(1,128)} %copy.17), calls=%async_computation | async-start | bytes 4096 | tf_op jit(solution)/shard_map/all_to_all | solution.py:677
  61.9 27.0 %collective-permute-start.3 = (bf16[32,8192]{1,0:T(8,128)(2,1)}, bf16[32,8192]{1,0:T(8,128)(2,1)S(1)}, u32[]{:S(2)}, u32[]{:S(2)}) collective-permute-start(bf16[32,8192]{1,0:T(8,128)(2,1)} %collective-permute-done.1.refs_2_), channel_id=1, source_target_pairs={{1,0},{2,3},{5,4},{6,7},{9,8},{10,11},{13,12},{14,15},{17,16},{18,... | collective-permute-start | bytes 1572872 | tf_op jit(solution)/shard_map/ppermute | solution.py:689
  63.2 10.8 %copy-start.13 = (bf16[32,8192]{1,0:T(8,128)(2,1)}, bf16[32,8192]{1,0:T(8,128)(2,1)S(1)}, u32[]{:S(2)}) copy-start(bf16[32,8192]{1,0:T(8,128)(2,1)S(1)} %collective-permute-done.2.refs_3_) | copy-start | bytes 1572868
  63.2 38.2 %collective-permute-start.4 = (bf16[32,8192]{1,0:T(8,128)(2,1)S(1)}, bf16[32,8192]{1,0:T(8,128)(2,1)}, u32[]{:S(2)}, u32[]{:S(2)}) collective-permute-start(bf16[32,8192]{1,0:T(8,128)(2,1)S(1)} %collective-permute-done.2.refs_3_), channel_id=1, source_target_pairs={{1,0},{2,3},{5,4},{6,7},{9,8},{10,11},{13,12},{14,15},{17,16},{18,... | collective-permute-start | bytes 1572872 | tf_op jit(solution)/shard_map/ppermute | solution.py:690
  64.6 76.4 %collective-permute-start.12 = (bf16[64,8192]{1,0:T(8,128)(2,1)}, bf16[64,8192]{1,0:T(8,128)(2,1)}, u32[]{:S(2)}, u32[]{:S(2)}) collective-permute-start(bf16[64,8192]{1,0:T(8,128)(2,1)} %collective-permute-done.11.refs_2_), channel_id=1, source_target_pairs={{1,0},{2,3},{5,4},{6,7},{9,8},{10,11},{13,12},{14,15},{17,16},{18,... | collective-permute-start | bytes 3145736 | tf_op jit(solution)/shard_map/ppermute | solution.py:707
  65.9 88.4 %collective-permute-start.20 = (bf16[64,8192]{1,0:T(8,128)(2,1)}, bf16[64,8192]{1,0:T(8,128)(2,1)}, u32[]{:S(2)}, u32[]{:S(2)}) collective-permute-start(bf16[64,8192]{1,0:T(8,128)(2,1)} %collective-permute-done.19.refs_2_), channel_id=1, source_target_pairs={{1,0},{2,3},{5,4},{6,7},{9,8},{10,11},{13,12},{14,15},{17,16},{18,... | collective-permute-start | bytes 3145736 | tf_op jit(solution)/shard_map/ppermute | solution.py:707
  74.0 5.8 %copy-start = (bf16[1024,8192]{1,0:T(8,128)(2,1)}, bf16[1024,8192]{1,0:T(8,128)(2,1)S(1)}, u32[]{:S(2)}) copy-start(bf16[1024,8192]{1,0:T(8,128)(2,1)S(1)} %load.3.out_w_ref) | copy-start | bytes 50331652
  80.2 29.0 %slice-start = ((s8[16777216]{0:T(1024)(128)(4,1)}), s8[4194304]{0:T(1024)(128)(4,1)S(1)}, s32[]{:S(2)}) async-start(s8[16777216]{0:T(1024)(128)(4,1)} %bitcast.4), calls=%async_computation.1 | async-start | bytes 8388608
  80.2 29.0 %slice-start.1 = ((s8[16777216]{0:T(1024)(128)(4,1)}), s8[4194304]{0:T(1024)(128)(4,1)S(1)}, s32[]{:S(2)}) async-start(s8[16777216]{0:T(1024)(128)(4,1)} %bitcast.4), calls=%async_computation.2 | async-start | bytes 8388608
  87.4 21.9 %copy-start.1 = (bf16[8192,1024]{1,0:T(8,128)(2,1)}, bf16[8192,1024]{1,0:T(8,128)(2,1)S(1)}, u32[]{:S(2)}) copy-start(bf16[8192,1024]{1,0:T(8,128)(2,1)S(1)} %get-tuple-element.32.refs_6_.refs_4_) | copy-start | bytes 50331652
  87.4 75.6 %collective-permute-start.28 = (bf16[64,8192]{1,0:T(8,128)(2,1)}, bf16[64,8192]{1,0:T(8,128)(2,1)S(1)}, u32[]{:S(2)}, u32[]{:S(2)}) collective-permute-start(bf16[64,8192]{1,0:T(8,128)(2,1)} %collective-permute-done.27.refs_2_), channel_id=1, source_target_pairs={{1,0},{2,3},{5,4},{6,7},{9,8},{10,11},{13,12},{14,15},{17,16},{18,... | collective-permute-start | bytes 3145736 | tf_op jit(solution)/shard_map/ppermute | solution.py:707
  89.0 12.4 %copy-start.14 = (bf16[32,8192]{1,0:T(8,128)(2,1)}, bf16[32,8192]{1,0:T(8,128)(2,1)S(1)}, u32[]{:S(2)}) copy-start(bf16[32,8192]{1,0:T(8,128)(2,1)S(1)} %collective-permute-done.3.refs_4_) | copy-start | bytes 1572868
  101.4 7.9 %slice-start.2 = ((s8[16777216]{0:T(1024)(128)(4,1)}), s8[4194304]{0:T(1024)(128)(4,1)S(1)}, s32[]{:S(2)}) async-start(s8[16777216]{0:T(1024)(128)(4,1)} %bitcast.4), calls=%async_computation.3 | async-start | bytes 8388608
  101.4 7.9 %slice-start.3 = ((s8[16777216]{0:T(1024)(128)(4,1)}), s8[4194304]{0:T(1024)(128)(4,1)S(1)}, s32[]{:S(2)}) async-start(s8[16777216]{0:T(1024)(128)(4,1)} %bitcast.4), calls=%async_computation.4 | async-start | bytes 8388608
  118.4 73.0 %collective-permute-start.5 = (bf16[64,8192]{1,0:T(8,128)(2,1)S(1)}, bf16[64,8192]{1,0:T(8,128)(2,1)S(1)}, u32[]{:S(2)}, u32[]{:S(2)}) collective-permute-start(bf16[64,8192]{1,0:T(8,128)(2,1)S(1)} %get-tuple-element.37), channel_id=1, source_target_pairs={{0,1},{3,2},{4,5},{7,6},{8,9},{11,10},{12,13},{15,14},{16,17},{19,... | collective-permute-start | bytes 3145736 | tf_op jit(solution)/shard_map/ppermute | solution.py:748
  139.5 132.2 %collective-permute-start.7 = (bf16[32,8192]{1,0:T(8,128)(2,1)S(1)}, bf16[32,8192]{1,0:T(8,128)(2,1)S(1)}, u32[]{:S(2)}, u32[]{:S(2)}) collective-permute-start(bf16[32,8192]{1,0:T(8,128)(2,1)S(1)} %get-tuple-element.38), channel_id=1, source_target_pairs={{0,1},{3,2},{4,5},{7,6},{8,9},{11,10},{12,13},{15,14},{16,17},{19,... | collective-permute-start | bytes 1572872 | tf_op jit(solution)/shard_map/ppermute | solution.py:750
  141.0 5.8 %copy-start.2 = (bf16[8192,1024]{1,0:T(8,128)(2,1)S(1)}, bf16[8192,1024]{1,0:T(8,128)(2,1)}, u32[]{:S(2)}) copy-start(bf16[8192,1024]{1,0:T(8,128)(2,1)} %copy-done.1) | copy-start | bytes 50331652
  163.0 1.0 copy-start.11
  177.8 22.3 %collective-permute-start.32 = (bf16[32,8192]{1,0:T(8,128)(2,1)S(1)}, bf16[32,8192]{1,0:T(8,128)(2,1)S(1)}, u32[]{:S(2)}, u32[]{:S(2)}) collective-permute-start(bf16[32,8192]{1,0:T(8,128)(2,1)S(1)} %get-tuple-element.59), channel_id=1, source_target_pairs={{0,1},{3,2},{4,5},{7,6},{8,9},{11,10},{12,13},{15,14},{16,17},{19,... | collective-permute-start | bytes 1572872 | tf_op jit(solution)/shard_map/ppermute | solution.py:739
  179.4 22.2 %collective-permute-start.30 = (bf16[32,8192]{1,0:T(8,128)(2,1)S(1)}, bf16[32,8192]{1,0:T(8,128)(2,1)S(1)}, u32[]{:S(2)}, u32[]{:S(2)}) collective-permute-start(bf16[32,8192]{1,0:T(8,128)(2,1)S(1)} %get-tuple-element.60), channel_id=1, source_target_pairs={{0,1},{3,2},{4,5},{7,6},{8,9},{11,10},{12,13},{15,14},{16,17},{19,... | collective-permute-start | bytes 1572872 | tf_op jit(solution)/shard_map/ppermute | solution.py:740
  180.7 233.2 %collective-permute-start.29 = (bf16[32,8192]{1,0:T(8,128)(2,1)S(1)}, bf16[32,8192]{1,0:T(8,128)(2,1)S(1)}, u32[]{:S(2)}, u32[]{:S(2)}) collective-permute-start(bf16[32,8192]{1,0:T(8,128)(2,1)S(1)} %get-tuple-element.58), channel_id=1, source_target_pairs={{0,1},{3,2},{4,5},{7,6},{8,9},{11,10},{12,13},{15,14},{16,17},{19,... | collective-permute-start | bytes 1572872 | tf_op jit(solution)/shard_map/ppermute | solution.py:741
  191.4 43.3 %collective-permute-start.21 = (bf16[64,8192]{1,0:T(8,128)(2,1)S(1)}, bf16[64,8192]{1,0:T(8,128)(2,1)S(1)}, u32[]{:S(2)}, u32[]{:S(2)}) collective-permute-start(bf16[64,8192]{1,0:T(8,128)(2,1)S(1)} %get-tuple-element.51), channel_id=1, source_target_pairs={{0,1},{3,2},{4,5},{7,6},{8,9},{11,10},{12,13},{15,14},{16,17},{19,... | collective-permute-start | bytes 3145736 | tf_op jit(solution)/shard_map/ppermute | solution.py:748
  200.1 127.2 %collective-permute-start.23 = (bf16[32,8192]{1,0:T(8,128)(2,1)S(1)}, bf16[32,8192]{1,0:T(8,128)(2,1)S(1)}, u32[]{:S(2)}, u32[]{:S(2)}) collective-permute-start(bf16[32,8192]{1,0:T(8,128)(2,1)S(1)} %get-tuple-element.52), channel_id=1, source_target_pairs={{0,1},{3,2},{4,5},{7,6},{8,9},{11,10},{12,13},{15,14},{16,17},{19,... | collective-permute-start | bytes 1572872 | tf_op jit(solution)/shard_map/ppermute | solution.py:750
  201.6 66.8 %collective-permute-start.13 = (bf16[64,8192]{1,0:T(8,128)(2,1)S(1)}, bf16[64,8192]{1,0:T(8,128)(2,1)S(1)}, u32[]{:S(2)}, u32[]{:S(2)}) collective-permute-start(bf16[64,8192]{1,0:T(8,128)(2,1)S(1)} %get-tuple-element.44), channel_id=1, source_target_pairs={{0,1},{3,2},{4,5},{7,6},{8,9},{11,10},{12,13},{15,14},{16,17},{19,... | collective-permute-start | bytes 3145736 | tf_op jit(solution)/shard_map/ppermute | solution.py:748
  234.7 159.4 %collective-permute-start.15 = (bf16[32,8192]{1,0:T(8,128)(2,1)S(1)}, bf16[32,8192]{1,0:T(8,128)(2,1)S(1)}, u32[]{:S(2)}, u32[]{:S(2)}) collective-permute-start(bf16[32,8192]{1,0:T(8,128)(2,1)S(1)} %get-tuple-element.45), channel_id=1, source_target_pairs={{0,1},{3,2},{4,5},{7,6},{8,9},{11,10},{12,13},{15,14},{16,17},{19,... | collective-permute-start | bytes 1572872 | tf_op jit(solution)/shard_map/ppermute | solution.py:750
  268.4 1.0 collective-permute-start.6
  269.4 0.8 collective-permute-start.33
  270.3 53.8 %collective-permute-start.8 = (bf16[32,8192]{1,0:T(8,128)(2,1)S(1)}, bf16[32,8192]{1,0:T(8,128)(2,1)S(1)}, u32[]{:S(2)}, u32[]{:S(2)}) collective-permute-start(bf16[32,8192]{1,0:T(8,128)(2,1)S(1)} %add_convert_fusion.11), channel_id=1, source_target_pairs={{1,0},{2,3},{5,4},{6,7},{9,8},{10,11},{13,12},{14,15},{17,16},{18,... | collective-permute-start | bytes 1572872 | tf_op jit(solution)/shard_map/ppermute | solution.py:752
  271.7 142.3 %collective-permute-start.31 = (bf16[32,8192]{1,0:T(8,128)(2,1)S(1)}, bf16[32,8192]{1,0:T(8,128)(2,1)S(1)}, u32[]{:S(2)}, u32[]{:S(2)}) collective-permute-start(bf16[32,8192]{1,0:T(8,128)(2,1)S(1)} %add_convert_fusion.5), channel_id=1, source_target_pairs={{1,2},{2,1},{5,6},{6,5},{9,10},{10,9},{13,14},{14,13},{17,18},{18,... | collective-permute-start | bytes 1572872 | tf_op jit(solution)/shard_map/ppermute | solution.py:743
  324.0 1.0 collective-permute-start.22
  325.0 0.9 collective-permute-start.14
  325.9 66.7 %collective-permute-start.24 = (bf16[32,8192]{1,0:T(8,128)(2,1)S(1)}, bf16[32,8192]{1,0:T(8,128)(2,1)S(1)}, u32[]{:S(2)}, u32[]{:S(2)}) collective-permute-start(bf16[32,8192]{1,0:T(8,128)(2,1)S(1)} %add_convert_fusion.7), channel_id=1, source_target_pairs={{1,0},{2,3},{5,4},{6,7},{9,8},{10,11},{13,12},{14,15},{17,16},{18,... | collective-permute-start | bytes 1572872 | tf_op jit(solution)/shard_map/ppermute | solution.py:752
  327.3 86.7 %collective-permute-start.34 = (bf16[32,8192]{1,0:T(8,128)(2,1)S(1)}, bf16[32,8192]{1,0:T(8,128)(2,1)S(1)}, u32[]{:S(2)}, u32[]{:S(2)}) collective-permute-start(bf16[32,8192]{1,0:T(8,128)(2,1)S(1)} %add_convert_fusion.3), channel_id=1, source_target_pairs={{1,0},{2,3},{5,4},{6,7},{9,8},{10,11},{13,12},{14,15},{17,16},{18,... | collective-permute-start | bytes 1572872 | tf_op jit(solution)/shard_map/ppermute | solution.py:744
  392.6 21.0 %collective-permute-start.16 = (bf16[32,8192]{1,0:T(8,128)(2,1)S(1)}, bf16[32,8192]{1,0:T(8,128)(2,1)S(1)}, u32[]{:S(2)}, u32[]{:S(2)}) collective-permute-start(bf16[32,8192]{1,0:T(8,128)(2,1)S(1)} %add_convert_fusion.9), channel_id=1, source_target_pairs={{1,0},{2,3},{5,4},{6,7},{9,8},{10,11},{13,12},{14,15},{17,16},{18,... | collective-permute-start | bytes 1572872 | tf_op jit(solution)/shard_map/ppermute | solution.py:752
  394.1 19.9 %collective-permute-start.9 = (bf16[32,8192]{1,0:T(8,128)(2,1)S(1)}, bf16[32,8192]{1,0:T(8,128)(2,1)S(1)}, u32[]{:S(2)}, u32[]{:S(2)}) collective-permute-start(bf16[32,8192]{1,0:T(8,128)(2,1)S(1)} %add_convert_fusion.10), channel_id=1, source_target_pairs={{0,12},{4,8},{8,4},{12,0},{1,13},{5,9},{9,5},{13,1},{2,14},{6,10},... | collective-permute-start | bytes 1572872 | tf_op jit(solution)/shard_map/ppermute | solution.py:755
  413.6 1.9 collective-permute-start.25
  413.9 14.4 %collective-permute-start.17 = (bf16[32,8192]{1,0:T(8,128)(2,1)S(1)}, bf16[32,8192]{1,0:T(8,128)(2,1)S(1)}, u32[]{:S(2)}, u32[]{:S(2)}) collective-permute-start(bf16[32,8192]{1,0:T(8,128)(2,1)S(1)} %add_convert_fusion.8), channel_id=1, source_target_pairs={{0,8},{4,12},{8,0},{12,4},{1,9},{5,13},{9,1},{13,5},{2,10},{6,14},... | collective-permute-start | bytes 1572872 | tf_op jit(solution)/shard_map/ppermute | solution.py:755
